TPU v7x, 256 devices: a whole 4x4x8 slice. The times are simulated.
256 devices in a mesh: gx: 8 (over z), gy: 32 (over x, y, core).
Axes of the slice: x: 4, y: 4, z: 8, core: 2. Of those that a mesh axis runs over, the one named last changes fastest.
Arguments:
- offsets: float32 [2, 16, 512, 128], P(None, 'gx', 'gy'), may hold values from 0 to 1
- density: float32 [16, 512, 128], P('gx', 'gy'), may hold values from 0.99 to 1.01
- velocity: float32 [2, 16, 512, 128], P(None, 'gx', 'gy'), may hold values from -4 to 4
- counts: int32 [16, 512], P('gx', 'gy'), may hold values from 1 to 128
- walls: int32 [16, 512], P('gx', 'gy'), may hold values 0 or 1
Outputs:
- new_offsets: float32 [2, 16, 512, 128], P(None, 'gx', 'gy')
- new_density: float32 [16, 512, 128], P('gx', 'gy')
- new_velocity: float32 [2, 16, 512, 128], P(None, 'gx', 'gy')
All inputs are finite; a program needn't handle non-finite values. No bound on the sum of `walls` on one device may be relied on, other than what follows from the above.
Results may differ from a plain program's by a relative error of at most 0.0001.
Values sent between devices are 32-bit elements; how exact they have to be, the bound alone decides.
A program may use at most 64 MiB of HBM per device.

v0:
```python
import functools
import math

import jax
import jax.numpy as jnp
from jax import lax
from jax.sharding import Mesh
from jax.sharding import PartitionSpec as P

ITERS = 3
GX_GY = ("gx", "gy_0", "gy_1", "gy_2")
GY = ("gy_0", "gy_1", "gy_2")


sound_speed = 10.0
stiffness = 100.0
courant = 0.2
smoothing = 0.1625
volume = 1.0 / 64.0
kernel_norm = 7.0 / (4.0 * math.pi * smoothing * smoothing)
grad_coef = -5.0 * kernel_norm / (smoothing * smoothing)
regular_sq = 0.01 * smoothing * smoothing
gravity_accel = 9.81


def extended(cells, sides, width):
    for axis, dim in sides:
        count = lax.axis_size(axis)
        ends = count - 1
        head = lax.slice_in_dim(cells, 0, width, axis=dim)
        tail = lax.slice_in_dim(cells, cells.shape[dim] - width, cells.shape[dim], axis=dim)
        cells = jnp.concatenate(
            [
                lax.ppermute(tail, axis, [(i, (i + 1) % count) for i in range(ends)]),
                cells,
                lax.ppermute(head, axis, [((i + 1) % count, i) for i in range(ends)]),
            ],
            axis=dim,
        )
    return cells


def by_axis(array, axes):
    return functools.reduce(lax.pmax, axes, array)


def pair_rates(fields, occ_pad):
    rows = fields.shape[1] - 2
    width = fields.shape[2] - 2

    def one_row(row_index):
        block = lax.dynamic_slice_in_dim(fields, row_index, 3, 1)
        occ_block = lax.dynamic_slice_in_dim(occ_pad, row_index, 3, 0)
        own = block[:, 1, 1 : width + 1]
        own_occ = occ_block[1, 1 : width + 1]
        own_rho = own[2] + 1.0 - own_occ
        total_rho = jnp.zeros(own[0].shape, jnp.float32)
        total_x = jnp.zeros(own[0].shape, jnp.float32)
        total_y = jnp.zeros(own[0].shape, jnp.float32)
        for shift_x in (-1, 0, 1):
            for shift_y in (-1, 0, 1):
                other = block[:, 1 + shift_x, 1 + shift_y : 1 + shift_y + width]
                other_occ = occ_block[1 + shift_x, 1 + shift_y : 1 + shift_y + width]
                weight = volume * other_occ / (other[2] + 1.0 - other_occ)
                delta_x = own[0][:, :, None] - other[0][:, None, :] - float(shift_x)
                delta_y = own[1][:, :, None] - other[1][:, None, :] - float(shift_y)
                dist_sq = delta_x * delta_x + delta_y * delta_y
                dist = jnp.sqrt(dist_sq)
                support = jnp.maximum(1.0 - 0.5 * dist / smoothing, 0.0)
                grad_mag = grad_coef * support * support * support
                rel_x = own[3][:, :, None] - other[3][:, None, :]
                rel_y = own[4][:, :, None] - other[4][:, None, :]
                along = rel_x * delta_x + rel_y * delta_y
                jump = own[5][:, :, None] - other[5][:, None, :]
                mean_p = 0.5 * (own[5][:, :, None] + other[5][:, None, :])
                scaled = grad_mag * weight[:, None, :]
                total_rho = total_rho + jnp.sum(
                    scaled * (0.5 * along - jump * dist / (2.0 * sound_speed)), -1
                )
                star = mean_p - 0.5 * sound_speed * along / jnp.sqrt(dist_sq + regular_sq)
                force = scaled * star
                total_x = total_x + jnp.sum(force * delta_x, -1)
                total_y = total_y + jnp.sum(force * delta_y, -1)
        return jnp.stack(
            [2.0 * own[2] * total_rho, -2.0 * total_x / own_rho, -2.0 * total_y / own_rho]
        )

    result = lax.map(one_row, jnp.arange(rows, dtype=jnp.int32))
    return jnp.transpose(result, (1, 0, 2, 3))


def shards(offsets, density, velocity, counts, walls):
    slots = density.shape[-1]
    counts_pad = extended(counts, (("gx", 0), (GY, 1)), 1)
    occ_pad = (
        lax.broadcasted_iota(jnp.int32, counts_pad.shape + (slots,), 2) < counts_pad[:, :, None]
    ).astype(jnp.float32)
    occupied = occ_pad[1:-1, 1:-1]
    keep = (1 - walls).astype(jnp.float32)[None, :, :, None]
    gravity = jnp.array([0.0, -gravity_accel], jnp.float32)[:, None, None, None]
    positions = offsets
    dens_now = density
    vel_now = velocity * keep
    for substep in range(ITERS):
        speed = jnp.sqrt(vel_now[0] * vel_now[0] + vel_now[1] * vel_now[1])
        local_top = jnp.max(sound_speed + occupied * speed)
        top_speed = by_axis(local_top, GX_GY)
        step_size = courant * smoothing / top_speed
        stacked = jnp.concatenate([positions, dens_now[None], vel_now], 0)
        padded = extended(stacked, (("gx", 1), (GY, 2)), 1)
        fields = jnp.concatenate([padded, stiffness * (padded[2:3] - 1.0)], 0)
        rates = pair_rates(fields, occ_pad)
        dens_now = dens_now + step_size * occupied * rates[0]
        vel_now = (vel_now + step_size * occupied[None] * (rates[1:3] + gravity)) * keep
        positions = positions + step_size * occupied[None] * vel_now
    return (positions, dens_now, vel_now)


def solution(mesh):
    split = Mesh(mesh.devices.reshape(mesh.shape["gx"], 4, 4, 2), ("gx", "gy_0", "gy_1", "gy_2"))
    return jax.shard_map(
        shards,
        mesh=split,
        in_specs=(
            P(None, "gx", GY, None),
            P("gx", GY, None),
            P(None, "gx", GY, None),
            P("gx", GY),
            P("gx", GY),
        ),
        out_specs=(P(None, "gx", GY, None), P("gx", GY, None), P(None, "gx", GY, None)),
        check_vma=False,
    )
```

profile of v0, /device:TPU:1, one launch (start us, length us, event | category | flops | bytes accessed | tf_op | source)
XLA Modules:
  0.0 336.0 jit_solution(8219685613974598456)
XLA Ops:
  0.6 0.7 subtract_convert_fusion
  1.3 0.8 broadcast_multiply_fusion
  2.2 4.4 %collective-permute-start.4 = (f32[5,1,16,128]{3,2,1,0:T(8,128)S(1)}, f32[5,1,16,128]{3,2,1,0:T(8,128)S(1)}, u32[]{:S(2)}, u32[]{:S(2)}) collective-permute-start(f32[5,1,16,128]{3,2,1,0:T(8,128)S(1)} %get-tuple-element.670), channel_id=1, source_target_pairs={{0,32},{32,64},{64,96},{96,128},{128,160},{160,192},{192,224},{1,3... | collective-permute-start | bytes 122888 | tf_op jit(solution)/shard_map/ppermute | solution.py:34
  6.6 1.3 collective-permute-start.5
  7.9 4.2 %collective-permute-start = (s32[1,16]{1,0:T(1,128)S(1)}, s32[1,16]{1,0:T(1,128)S(1)}, u32[]{:S(2)}, u32[]{:S(2)}) collective-permute-start(s32[1,16]{1,0:T(1,128)S(1)} %get-tuple-element.674), channel_id=1, source_target_pairs={{0,32},{32,64},{64,96},{96,128},{128,160},{160,192},{192,224},{1,3... | collective-permute-start | bytes 200 | tf_op jit(solution)/shard_map/ppermute | solution.py:34
  12.1 1.3 collective-permute-start.1
  13.4 3.2 collective-permute-done.1
  16.7 5.4 %collective-permute-start.2 = (s32[4,1]{1,0:T(4,128)S(1)}, s32[4,1]{1,0:T(4,128)S(1)}, u32[]{:S(2)}, u32[]{:S(2)}) collective-permute-start(s32[4,1]{1,0:T(4,128)S(1)} %get-tuple-element.672), channel_id=1, source_target_pairs={{0,1},{1,2},{2,3},{3,4},{4,5},{5,6},{6,7},{7,8},{8,9},{9,10},{10,1... | collective-permute-start | bytes 56 | tf_op jit(solution)/shard_map/ppermute | solution.py:34
  22.0 1.9 collective-permute-start.3
  24.0 3.0 collective-permute-done.3
  27.2 2.0 collective-permute-start.6
  29.1 2.4 collective-permute-start.7
  32.1 17.4 %pmax.84 = f32[]{:T(128)} all-reduce(f32[]{:T(128)} %fusion.417), channel_id=1, replica_groups=mesh['gx'=8,'gy_0'=4,'gy_1'=4,'gy_2'=2] {'gx'}, use_global_device_ids=true, to_apply=%region_1.0 | all-reduce | flops 1 | bytes 8 | tf_op jit(solution)/shard_map/pmax | solution.py:44
  49.5 9.6 %pmax.85 = f32[]{:T(128)} all-reduce(f32[]{:T(128)} %pmax.84), channel_id=1, replica_groups=mesh['gx'=8,'gy_0'=4,'gy_1'=4,'gy_2'=2] {'gy_0'}, use_global_device_ids=true, to_apply=%region_2.0 | all-reduce | flops 1 | bytes 8 | tf_op jit(solution)/shard_map/pmax | solution.py:44
  59.1 9.0 %pmax.86 = f32[]{:T(128)} all-reduce(f32[]{:T(128)} %pmax.85), channel_id=1, replica_groups=mesh['gx'=8,'gy_0'=4,'gy_1'=4,'gy_2'=2] {'gy_1'}, use_global_device_ids=true, to_apply=%region_3.0 | all-reduce | flops 1 | bytes 8 | tf_op jit(solution)/shard_map/pmax | solution.py:44
  68.1 11.4 %pmax.87 = f32[]{:T(128)} all-reduce(f32[]{:T(128)} %pmax.86), channel_id=1, replica_groups=mesh['gx'=8,'gy_0'=4,'gy_1'=4,'gy_2'=2] {'gy_2'}, use_global_device_ids=true, to_apply=%region_4.0 | all-reduce | flops 1 | bytes 8 | tf_op jit(solution)/shard_map/pmax | solution.py:44
  80.3 46.4 %while.39 = (s32[]{:T(128)}, f32[2,3,16,128]{3,2,0,1:T(8,128)S(1)}, s32[2]{0:T(128)S(1)}, f32[6,4,18,128]{3,2,1,0:T(8,128)S(1)}, f32[4,18,128]{2,1,0:T(8,128)S(1...) while((s32[]{:T(128)}, f32[2,3,16,128]{3,2,0,1:T(8,128)S(1)}, ...), condition=%wide.region_33.34_spmd, body=%wide.region_5.33_spmd.sunk | while | flops 85821456 | bytes 2081115 | solution.py:88
  83.2 4.6 %multiply_reduce_fusion.75 = (f32[16,128]{1,0:T(8,128)S(1)}, f32[16,128]{1,0:T(8,128)S(1)}, f32[16,128]{1,0:T(8,128)S(1)}, f32[16,128]{1,0:T(8,128)S(1)}, f32[16,128]{1,0:T(8,128)S(1)}, /*index=5*/f32[16,128]{1,0:T(8,128)S(1)}) fusion(f32[16,128]{1,0:T(8,128)S(1)} %get-tuple-element.1049, f32[16,128]{1,0:T(8,128)S(1)} %get-tuple-element.1008, ...), kind=kLoop, calls=%fused_computation.108.clone.1 | loop fusion | flops 19124224 | bytes 188416 | tf_op jit(solution)/shard_map/while/body/eval_jaxpr/reduce_sum | solution.py:77
  87.8 6.4 %multiply_reduce_fusion.74 = (f32[16,128]{1,0:T(8,128)S(1)}, f32[16,128]{1,0:T(8,128)S(1)}, f32[16,128]{1,0:T(8,128)S(1)}, f32[16,128]{1,0:T(8,128)S(1)}, f32[16...) fusion(f32[16,128]{1,0:T(8,128)S(1)} %get-tuple-element.1035, ...), kind=kLoop, calls=%fused_computation.106.clone.1 | loop fusion | flops 28293120 | bytes 221184 | tf_op jit(solution)/shard_map/while/body/eval_jaxpr/reduce_sum | solution.py:77
  94.2 4.6 %multiply_reduce_fusion.73 = (f32[16,128]{1,0:T(8,128)S(1)}, f32[16,128]{1,0:T(8,128)S(1)}, f32[16,128]{1,0:T(8,128)S(1)}, f32[16,128]{1,0:T(8,128)S(1)}, f32[16,128]{1,0:T(8,128)S(1)}, /*index=5*/f32[16,128]{1,0:T(8,128)S(1)}) fusion(f32[16,128]{1,0:T(8,128)S(1)} %get-tuple-element.1021, f32[16,128]{1,0:T(8,128)S(1)} %get-tuple-element.1022, ...), kind=kLoop, calls=%fused_computation.97.clone.1 | loop fusion | flops 19124224 | bytes 188416 | tf_op jit(solution)/shard_map/while/body/eval_jaxpr/reduce_sum | solution.py:77
  98.8 4.6 %multiply_reduce_fusion.72 = (f32[16,128]{1,0:T(8,128)S(1)}, f32[16,128]{1,0:T(8,128)S(1)}, f32[16,128]{1,0:T(8,128)S(1)}, f32[16,128]{1,0:T(8,128)S(1)}, f32[16,128]{1,0:T(8,128)S(1)}, /*index=5*/f32[16,128]{1,0:T(8,128)S(1)}) fusion(f32[16,128]{1,0:T(8,128)S(1)} %get-tuple-element.1002, f32[16,128]{1,0:T(8,128)S(1)} %get-tuple-element.1003, ...), kind=kLoop, calls=%fused_computation.90.clone.1 | loop fusion | flops 19124224 | bytes 188416 | tf_op jit(solution)/shard_map/while/body/eval_jaxpr/reduce_sum | solution.py:77
  106.4 4.6 %multiply_reduce_fusion.75 = (f32[16,128]{1,0:T(8,128)S(1)}, f32[16,128]{1,0:T(8,128)S(1)}, f32[16,128]{1,0:T(8,128)S(1)}, f32[16,128]{1,0:T(8,128)S(1)}, f32[16,128]{1,0:T(8,128)S(1)}, /*index=5*/f32[16,128]{1,0:T(8,128)S(1)}) fusion(f32[16,128]{1,0:T(8,128)S(1)} %get-tuple-element.1049, f32[16,128]{1,0:T(8,128)S(1)} %get-tuple-element.1008, ...), kind=kLoop, calls=%fused_computation.108.clone.1 | loop fusion | flops 19124224 | bytes 188416 | tf_op jit(solution)/shard_map/while/body/eval_jaxpr/reduce_sum | solution.py:77
  111.0 6.4 %multiply_reduce_fusion.74 = (f32[16,128]{1,0:T(8,128)S(1)}, f32[16,128]{1,0:T(8,128)S(1)}, f32[16,128]{1,0:T(8,128)S(1)}, f32[16,128]{1,0:T(8,128)S(1)}, f32[16...) fusion(f32[16,128]{1,0:T(8,128)S(1)} %get-tuple-element.1035, ...), kind=kLoop, calls=%fused_computation.106.clone.1 | loop fusion | flops 28293120 | bytes 221184 | tf_op jit(solution)/shard_map/while/body/eval_jaxpr/reduce_sum | solution.py:77
  117.4 4.6 %multiply_reduce_fusion.73 = (f32[16,128]{1,0:T(8,128)S(1)}, f32[16,128]{1,0:T(8,128)S(1)}, f32[16,128]{1,0:T(8,128)S(1)}, f32[16,128]{1,0:T(8,128)S(1)}, f32[16,128]{1,0:T(8,128)S(1)}, /*index=5*/f32[16,128]{1,0:T(8,128)S(1)}) fusion(f32[16,128]{1,0:T(8,128)S(1)} %get-tuple-element.1021, f32[16,128]{1,0:T(8,128)S(1)} %get-tuple-element.1022, ...), kind=kLoop, calls=%fused_computation.97.clone.1 | loop fusion | flops 19124224 | bytes 188416 | tf_op jit(solution)/shard_map/while/body/eval_jaxpr/reduce_sum | solution.py:77
  122.0 4.6 %multiply_reduce_fusion.72 = (f32[16,128]{1,0:T(8,128)S(1)}, f32[16,128]{1,0:T(8,128)S(1)}, f32[16,128]{1,0:T(8,128)S(1)}, f32[16,128]{1,0:T(8,128)S(1)}, f32[16,128]{1,0:T(8,128)S(1)}, /*index=5*/f32[16,128]{1,0:T(8,128)S(1)}) fusion(f32[16,128]{1,0:T(8,128)S(1)} %get-tuple-element.1002, f32[16,128]{1,0:T(8,128)S(1)} %get-tuple-element.1003, ...), kind=kLoop, calls=%fused_computation.90.clone.1 | loop fusion | flops 19124224 | bytes 188416 | tf_op jit(solution)/shard_map/while/body/eval_jaxpr/reduce_sum | solution.py:77
  126.8 0.7 copy-done.2
  127.6 1.4 collective-permute-start.8
  129.0 1.3 collective-permute-start.9
  130.3 4.0 %collective-permute-done.9 = f32[5,1,16,128]{3,2,1,0:T(8,128)S(1)} collective-permute-done((f32[5,1,16,128]{3,2,1,0:T(8,128)S(1)}, f32[5,1,16,128]{3,2,1,0:T(8,128)S(1)}, u32[]{:S(2)}, u32[]{:S(2)}) %collective-permute-start.9) | collective-permute-done | bytes 40992 | tf_op jit(solution)/shard_map/ppermute | solution.py:36
  134.3 5.0 %collective-permute-start.10 = (f32[5,4,1,128]{3,2,1,0:T(1,128)S(1)}, f32[5,4,1,128]{3,2,1,0:T(1,128)S(1)}, u32[]{:S(2)}, u32[]{:S(2)}) collective-permute-start(f32[5,4,1,128]{3,2,1,0:T(1,128)S(1)} %get-tuple-element.662), channel_id=1, source_target_pairs={{0,1},{1,2},{2,3},{3,4},{4,5},{5,6},{6,7},{7,8},{8,9},{9,10},{10,1... | collective-permute-start | bytes 30728 | tf_op jit(solution)/shard_map/ppermute | solution.py:34
  139.3 1.9 collective-permute-start.11
  141.9 15.9 %pmax.88 = f32[]{:T(128)} all-reduce(f32[]{:T(128)} %fusion.411), channel_id=1, replica_groups=mesh['gx'=8,'gy_0'=4,'gy_1'=4,'gy_2'=2] {'gx'}, use_global_device_ids=true, to_apply=%region_35.36 | all-reduce | flops 1 | bytes 8 | tf_op jit(solution)/shard_map/pmax | solution.py:44
  157.8 6.6 %pmax.89 = f32[]{:T(128)} all-reduce(f32[]{:T(128)} %pmax.88), channel_id=1, replica_groups=mesh['gx'=8,'gy_0'=4,'gy_1'=4,'gy_2'=2] {'gy_0'}, use_global_device_ids=true, to_apply=%region_36.37 | all-reduce | flops 1 | bytes 8 | tf_op jit(solution)/shard_map/pmax | solution.py:44
  164.4 7.0 %pmax.90 = f32[]{:T(128)} all-reduce(f32[]{:T(128)} %pmax.89), channel_id=1, replica_groups=mesh['gx'=8,'gy_0'=4,'gy_1'=4,'gy_2'=2] {'gy_1'}, use_global_device_ids=true, to_apply=%region_37.38 | all-reduce | flops 1 | bytes 8 | tf_op jit(solution)/shard_map/pmax | solution.py:44
  171.4 11.4 %pmax.91 = f32[]{:T(128)} all-reduce(f32[]{:T(128)} %pmax.90), channel_id=1, replica_groups=mesh['gx'=8,'gy_0'=4,'gy_1'=4,'gy_2'=2] {'gy_2'}, use_global_device_ids=true, to_apply=%region_38.39 | all-reduce | flops 1 | bytes 8 | tf_op jit(solution)/shard_map/pmax | solution.py:44
  183.6 46.4 %while.40 = (s32[]{:T(128)}, f32[2,3,16,128]{3,2,0,1:T(8,128)S(1)}, s32[2]{0:T(128)S(1)}, f32[6,4,18,128]{3,2,1,0:T(8,128)S(1)}, f32[4,18,128]{2,1,0:T(8,128)S(1...) while((s32[]{:T(128)}, f32[2,3,16,128]{3,2,0,1:T(8,128)S(1)}, ...), condition=%wide.region_67.68_spmd, body=%wide.region_39.67_spmd.sunk | while | flops 85821456 | bytes 2081115 | solution.py:88
  186.4 4.6 %multiply_reduce_fusion.79 = (f32[16,128]{1,0:T(8,128)S(1)}, f32[16,128]{1,0:T(8,128)S(1)}, f32[16,128]{1,0:T(8,128)S(1)}, f32[16,128]{1,0:T(8,128)S(1)}, f32[16,128]{1,0:T(8,128)S(1)}, /*index=5*/f32[16,128]{1,0:T(8,128)S(1)}) fusion(f32[16,128]{1,0:T(8,128)S(1)} %get-tuple-element.1135, f32[16,128]{1,0:T(8,128)S(1)} %get-tuple-element.1094, ...), kind=kLoop, calls=%fused_computation.379.clone.1 | loop fusion | flops 19124224 | bytes 188416 | tf_op jit(solution)/shard_map/while/body/eval_jaxpr/reduce_sum | solution.py:77
  191.1 6.4 %multiply_reduce_fusion.78 = (f32[16,128]{1,0:T(8,128)S(1)}, f32[16,128]{1,0:T(8,128)S(1)}, f32[16,128]{1,0:T(8,128)S(1)}, f32[16,128]{1,0:T(8,128)S(1)}, f32[16...) fusion(f32[16,128]{1,0:T(8,128)S(1)} %get-tuple-element.1121, ...), kind=kLoop, calls=%fused_computation.377.clone.1 | loop fusion | flops 28293120 | bytes 221184 | tf_op jit(solution)/shard_map/while/body/eval_jaxpr/reduce_sum | solution.py:77
  197.5 4.6 %multiply_reduce_fusion.77 = (f32[16,128]{1,0:T(8,128)S(1)}, f32[16,128]{1,0:T(8,128)S(1)}, f32[16,128]{1,0:T(8,128)S(1)}, f32[16,128]{1,0:T(8,128)S(1)}, f32[16,128]{1,0:T(8,128)S(1)}, /*index=5*/f32[16,128]{1,0:T(8,128)S(1)}) fusion(f32[16,128]{1,0:T(8,128)S(1)} %get-tuple-element.1107, f32[16,128]{1,0:T(8,128)S(1)} %get-tuple-element.1108, ...), kind=kLoop, calls=%fused_computation.368.clone.1 | loop fusion | flops 19124224 | bytes 188416 | tf_op jit(solution)/shard_map/while/body/eval_jaxpr/reduce_sum | solution.py:77
  202.1 4.6 %multiply_reduce_fusion.76 = (f32[16,128]{1,0:T(8,128)S(1)}, f32[16,128]{1,0:T(8,128)S(1)}, f32[16,128]{1,0:T(8,128)S(1)}, f32[16,128]{1,0:T(8,128)S(1)}, f32[16,128]{1,0:T(8,128)S(1)}, /*index=5*/f32[16,128]{1,0:T(8,128)S(1)}) fusion(f32[16,128]{1,0:T(8,128)S(1)} %get-tuple-element.1088, f32[16,128]{1,0:T(8,128)S(1)} %get-tuple-element.1089, ...), kind=kLoop, calls=%fused_computation.361.clone.1 | loop fusion | flops 19124224 | bytes 188416 | tf_op jit(solution)/shard_map/while/body/eval_jaxpr/reduce_sum | solution.py:77
  209.6 4.6 %multiply_reduce_fusion.79 = (f32[16,128]{1,0:T(8,128)S(1)}, f32[16,128]{1,0:T(8,128)S(1)}, f32[16,128]{1,0:T(8,128)S(1)}, f32[16,128]{1,0:T(8,128)S(1)}, f32[16,128]{1,0:T(8,128)S(1)}, /*index=5*/f32[16,128]{1,0:T(8,128)S(1)}) fusion(f32[16,128]{1,0:T(8,128)S(1)} %get-tuple-element.1135, f32[16,128]{1,0:T(8,128)S(1)} %get-tuple-element.1094, ...), kind=kLoop, calls=%fused_computation.379.clone.1 | loop fusion | flops 19124224 | bytes 188416 | tf_op jit(solution)/shard_map/while/body/eval_jaxpr/reduce_sum | solution.py:77
  214.3 6.4 %multiply_reduce_fusion.78 = (f32[16,128]{1,0:T(8,128)S(1)}, f32[16,128]{1,0:T(8,128)S(1)}, f32[16,128]{1,0:T(8,128)S(1)}, f32[16,128]{1,0:T(8,128)S(1)}, f32[16...) fusion(f32[16,128]{1,0:T(8,128)S(1)} %get-tuple-element.1121, ...), kind=kLoop, calls=%fused_computation.377.clone.1 | loop fusion | flops 28293120 | bytes 221184 | tf_op jit(solution)/shard_map/while/body/eval_jaxpr/reduce_sum | solution.py:77
  220.7 4.6 %multiply_reduce_fusion.77 = (f32[16,128]{1,0:T(8,128)S(1)}, f32[16,128]{1,0:T(8,128)S(1)}, f32[16,128]{1,0:T(8,128)S(1)}, f32[16,128]{1,0:T(8,128)S(1)}, f32[16,128]{1,0:T(8,128)S(1)}, /*index=5*/f32[16,128]{1,0:T(8,128)S(1)}) fusion(f32[16,128]{1,0:T(8,128)S(1)} %get-tuple-element.1107, f32[16,128]{1,0:T(8,128)S(1)} %get-tuple-element.1108, ...), kind=kLoop, calls=%fused_computation.368.clone.1 | loop fusion | flops 19124224 | bytes 188416 | tf_op jit(solution)/shard_map/while/body/eval_jaxpr/reduce_sum | solution.py:77
  225.3 4.6 %multiply_reduce_fusion.76 = (f32[16,128]{1,0:T(8,128)S(1)}, f32[16,128]{1,0:T(8,128)S(1)}, f32[16,128]{1,0:T(8,128)S(1)}, f32[16,128]{1,0:T(8,128)S(1)}, f32[16,128]{1,0:T(8,128)S(1)}, /*index=5*/f32[16,128]{1,0:T(8,128)S(1)}) fusion(f32[16,128]{1,0:T(8,128)S(1)} %get-tuple-element.1088, f32[16,128]{1,0:T(8,128)S(1)} %get-tuple-element.1089, ...), kind=kLoop, calls=%fused_computation.361.clone.1 | loop fusion | flops 19124224 | bytes 188416 | tf_op jit(solution)/shard_map/while/body/eval_jaxpr/reduce_sum | solution.py:77
  230.1 1.4 collective-permute-start.12
  231.5 1.3 collective-permute-start.13
  232.8 4.0 %collective-permute-done.13 = f32[5,1,16,128]{3,2,1,0:T(8,128)S(1)} collective-permute-done((f32[5,1,16,128]{3,2,1,0:T(8,128)S(1)}, f32[5,1,16,128]{3,2,1,0:T(8,128)S(1)}, u32[]{:S(2)}, u32[]{:S(2)}) %collective-permute-start.13) | collective-permute-done | bytes 40992 | tf_op jit(solution)/shard_map/ppermute | solution.py:36
  236.8 4.9 %collective-permute-start.14 = (f32[5,4,1,128]{3,2,1,0:T(1,128)S(1)}, f32[5,4,1,128]{3,2,1,0:T(1,128)S(1)}, u32[]{:S(2)}, u32[]{:S(2)}) collective-permute-start(f32[5,4,1,128]{3,2,1,0:T(1,128)S(1)} %get-tuple-element.660), channel_id=1, source_target_pairs={{0,1},{1,2},{2,3},{3,4},{4,5},{5,6},{6,7},{7,8},{8,9},{9,10},{10,1... | collective-permute-start | bytes 30728 | tf_op jit(solution)/shard_map/ppermute | solution.py:34
  241.7 1.9 collective-permute-start.15
  244.2 15.7 %pmax.92 = f32[]{:T(128)} all-reduce(f32[]{:T(128)} %fusion.403), channel_id=1, replica_groups=mesh['gx'=8,'gy_0'=4,'gy_1'=4,'gy_2'=2] {'gx'}, use_global_device_ids=true, to_apply=%region_69.70 | all-reduce | flops 1 | bytes 8 | tf_op jit(solution)/shard_map/pmax | solution.py:44
  260.0 6.6 %pmax.93 = f32[]{:T(128)} all-reduce(f32[]{:T(128)} %pmax.92), channel_id=1, replica_groups=mesh['gx'=8,'gy_0'=4,'gy_1'=4,'gy_2'=2] {'gy_0'}, use_global_device_ids=true, to_apply=%region_70.71 | all-reduce | flops 1 | bytes 8 | tf_op jit(solution)/shard_map/pmax | solution.py:44
  266.6 9.2 %pmax.94 = f32[]{:T(128)} all-reduce(f32[]{:T(128)} %pmax.93), channel_id=1, replica_groups=mesh['gx'=8,'gy_0'=4,'gy_1'=4,'gy_2'=2] {'gy_1'}, use_global_device_ids=true, to_apply=%region_71.72 | all-reduce | flops 1 | bytes 8 | tf_op jit(solution)/shard_map/pmax | solution.py:44
  275.8 11.7 %pmax.95 = f32[]{:T(128)} all-reduce(f32[]{:T(128)} %pmax.94), channel_id=1, replica_groups=mesh['gx'=8,'gy_0'=4,'gy_1'=4,'gy_2'=2] {'gy_2'}, use_global_device_ids=true, to_apply=%region_72.73 | all-reduce | flops 1 | bytes 8 | tf_op jit(solution)/shard_map/pmax | solution.py:44
  288.3 46.4 %while.41 = (s32[]{:T(128)}, f32[2,3,16,128]{3,2,0,1:T(8,128)S(1)}, s32[2]{0:T(128)S(1)}, f32[6,4,18,128]{3,2,1,0:T(8,128)S(1)}, f32[4,18,128]{2,1,0:T(8,128)S(1...) while((s32[]{:T(128)}, f32[2,3,16,128]{3,2,0,1:T(8,128)S(1)}, ...), condition=%wide.region_101.102_spmd, body=%wide.region_73.101_spmd.sunk | while | flops 85821456 | bytes 2081115 | solution.py:88
  291.1 4.6 %multiply_reduce_fusion.83 = (f32[16,128]{1,0:T(8,128)S(1)}, f32[16,128]{1,0:T(8,128)S(1)}, f32[16,128]{1,0:T(8,128)S(1)}, f32[16,128]{1,0:T(8,128)S(1)}, f32[16,128]{1,0:T(8,128)S(1)}, /*index=5*/f32[16,128]{1,0:T(8,128)S(1)}) fusion(f32[16,128]{1,0:T(8,128)S(1)} %get-tuple-element.1221, f32[16,128]{1,0:T(8,128)S(1)} %get-tuple-element.1180, ...), kind=kLoop, calls=%fused_computation.650.clone.1 | loop fusion | flops 19124224 | bytes 188416 | tf_op jit(solution)/shard_map/while/body/eval_jaxpr/reduce_sum | solution.py:77
  295.8 6.4 %multiply_reduce_fusion.82 = (f32[16,128]{1,0:T(8,128)S(1)}, f32[16,128]{1,0:T(8,128)S(1)}, f32[16,128]{1,0:T(8,128)S(1)}, f32[16,128]{1,0:T(8,128)S(1)}, f32[16...) fusion(f32[16,128]{1,0:T(8,128)S(1)} %get-tuple-element.1207, ...), kind=kLoop, calls=%fused_computation.648.clone.1 | loop fusion | flops 28293120 | bytes 221184 | tf_op jit(solution)/shard_map/while/body/eval_jaxpr/reduce_sum | solution.py:77
  302.2 4.6 %multiply_reduce_fusion.81 = (f32[16,128]{1,0:T(8,128)S(1)}, f32[16,128]{1,0:T(8,128)S(1)}, f32[16,128]{1,0:T(8,128)S(1)}, f32[16,128]{1,0:T(8,128)S(1)}, f32[16,128]{1,0:T(8,128)S(1)}, /*index=5*/f32[16,128]{1,0:T(8,128)S(1)}) fusion(f32[16,128]{1,0:T(8,128)S(1)} %get-tuple-element.1193, f32[16,128]{1,0:T(8,128)S(1)} %get-tuple-element.1194, ...), kind=kLoop, calls=%fused_computation.639.clone.1 | loop fusion | flops 19124224 | bytes 188416 | tf_op jit(solution)/shard_map/while/body/eval_jaxpr/reduce_sum | solution.py:77
  306.8 4.6 %multiply_reduce_fusion.80 = (f32[16,128]{1,0:T(8,128)S(1)}, f32[16,128]{1,0:T(8,128)S(1)}, f32[16,128]{1,0:T(8,128)S(1)}, f32[16,128]{1,0:T(8,128)S(1)}, f32[16,128]{1,0:T(8,128)S(1)}, /*index=5*/f32[16,128]{1,0:T(8,128)S(1)}) fusion(f32[16,128]{1,0:T(8,128)S(1)} %get-tuple-element.1174, f32[16,128]{1,0:T(8,128)S(1)} %get-tuple-element.1175, ...), kind=kLoop, calls=%fused_computation.632.clone.1 | loop fusion | flops 19124224 | bytes 188416 | tf_op jit(solution)/shard_map/while/body/eval_jaxpr/reduce_sum | solution.py:77
  314.3 4.6 %multiply_reduce_fusion.83 = (f32[16,128]{1,0:T(8,128)S(1)}, f32[16,128]{1,0:T(8,128)S(1)}, f32[16,128]{1,0:T(8,128)S(1)}, f32[16,128]{1,0:T(8,128)S(1)}, f32[16,128]{1,0:T(8,128)S(1)}, /*index=5*/f32[16,128]{1,0:T(8,128)S(1)}) fusion(f32[16,128]{1,0:T(8,128)S(1)} %get-tuple-element.1221, f32[16,128]{1,0:T(8,128)S(1)} %get-tuple-element.1180, ...), kind=kLoop, calls=%fused_computation.650.clone.1 | loop fusion | flops 19124224 | bytes 188416 | tf_op jit(solution)/shard_map/while/body/eval_jaxpr/reduce_sum | solution.py:77
  318.9 6.4 %multiply_reduce_fusion.82 = (f32[16,128]{1,0:T(8,128)S(1)}, f32[16,128]{1,0:T(8,128)S(1)}, f32[16,128]{1,0:T(8,128)S(1)}, f32[16,128]{1,0:T(8,128)S(1)}, f32[16...) fusion(f32[16,128]{1,0:T(8,128)S(1)} %get-tuple-element.1207, ...), kind=kLoop, calls=%fused_computation.648.clone.1 | loop fusion | flops 28293120 | bytes 221184 | tf_op jit(solution)/shard_map/while/body/eval_jaxpr/reduce_sum | solution.py:77
  325.4 4.6 %multiply_reduce_fusion.81 = (f32[16,128]{1,0:T(8,128)S(1)}, f32[16,128]{1,0:T(8,128)S(1)}, f32[16,128]{1,0:T(8,128)S(1)}, f32[16,128]{1,0:T(8,128)S(1)}, f32[16,128]{1,0:T(8,128)S(1)}, /*index=5*/f32[16,128]{1,0:T(8,128)S(1)}) fusion(f32[16,128]{1,0:T(8,128)S(1)} %get-tuple-element.1193, f32[16,128]{1,0:T(8,128)S(1)} %get-tuple-element.1194, ...), kind=kLoop, calls=%fused_computation.639.clone.1 | loop fusion | flops 19124224 | bytes 188416 | tf_op jit(solution)/shard_map/while/body/eval_jaxpr/reduce_sum | solution.py:77
  330.0 4.6 %multiply_reduce_fusion.80 = (f32[16,128]{1,0:T(8,128)S(1)}, f32[16,128]{1,0:T(8,128)S(1)}, f32[16,128]{1,0:T(8,128)S(1)}, f32[16,128]{1,0:T(8,128)S(1)}, f32[16,128]{1,0:T(8,128)S(1)}, /*index=5*/f32[16,128]{1,0:T(8,128)S(1)}) fusion(f32[16,128]{1,0:T(8,128)S(1)} %get-tuple-element.1174, f32[16,128]{1,0:T(8,128)S(1)} %get-tuple-element.1175, ...), kind=kLoop, calls=%fused_computation.632.clone.1 | loop fusion | flops 19124224 | bytes 188416 | tf_op jit(solution)/shard_map/while/body/eval_jaxpr/reduce_sum | solution.py:77
  334.7 0.6 fusion.395
  335.3 0.7 multiply_add_fusion.24
  (96 shorter events, 8.3 us)
Async XLA Ops:
  1.3 0.8 copy-start
  1.3 0.8 copy-start.1
  2.2 5.7 %copy-start.3 = (s32[2,16]{1,0:T(2,128)S(1)}, s32[2,16]{1,0:T(2,128)}, u32[]{:S(2)}) copy-start(s32[2,16]{1,0:T(2,128)} %param.15) | copy-start | bytes 388
  2.2 24.9 %collective-permute-start.4 = (f32[5,1,16,128]{3,2,1,0:T(8,128)S(1)}, f32[5,1,16,128]{3,2,1,0:T(8,128)S(1)}, u32[]{:S(2)}, u32[]{:S(2)}) collective-permute-start(f32[5,1,16,128]{3,2,1,0:T(8,128)S(1)} %get-tuple-element.670), channel_id=1, source_target_pairs={{0,32},{32,64},{64,96},{96,128},{128,160},{160,192},{192,224},{1,3... | collective-permute-start | bytes 122888 | tf_op jit(solution)/shard_map/ppermute | solution.py:34
  6.6 20.6 %collective-permute-start.5 = (f32[5,1,16,128]{3,2,1,0:T(8,128)S(1)}, f32[5,1,16,128]{3,2,1,0:T(8,128)S(1)}, u32[]{:S(2)}, u32[]{:S(2)}) collective-permute-start(f32[5,1,16,128]{3,2,1,0:T(8,128)S(1)} %get-tuple-element.671), channel_id=1, source_target_pairs={{32,0},{64,32},{96,64},{128,96},{160,128},{192,160},{224,192},{33,... | collective-permute-start | bytes 122888 | tf_op jit(solution)/shard_map/ppermute | solution.py:36
  7.9 5.5 %collective-permute-start = (s32[1,16]{1,0:T(1,128)S(1)}, s32[1,16]{1,0:T(1,128)S(1)}, u32[]{:S(2)}, u32[]{:S(2)}) collective-permute-start(s32[1,16]{1,0:T(1,128)S(1)} %get-tuple-element.674), channel_id=1, source_target_pairs={{0,32},{32,64},{64,96},{96,128},{128,160},{160,192},{192,224},{1,3... | collective-permute-start | bytes 200 | tf_op jit(solution)/shard_map/ppermute | solution.py:34
  12.1 4.5 %collective-permute-start.1 = (s32[1,16]{1,0:T(1,128)S(1)}, s32[1,16]{1,0:T(1,128)S(1)}, u32[]{:S(2)}, u32[]{:S(2)}) collective-permute-start(s32[1,16]{1,0:T(1,128)S(1)} %get-tuple-element.675), channel_id=1, source_target_pairs={{32,0},{64,32},{96,64},{128,96},{160,128},{192,160},{224,192},{33,... | collective-permute-start | bytes 200 | tf_op jit(solution)/shard_map/ppermute | solution.py:36
  16.7 7.3 %collective-permute-start.2 = (s32[4,1]{1,0:T(4,128)S(1)}, s32[4,1]{1,0:T(4,128)S(1)}, u32[]{:S(2)}, u32[]{:S(2)}) collective-permute-start(s32[4,1]{1,0:T(4,128)S(1)} %get-tuple-element.672), channel_id=1, source_target_pairs={{0,1},{1,2},{2,3},{3,4},{4,5},{5,6},{6,7},{7,8},{8,9},{9,10},{10,1... | collective-permute-start | bytes 56 | tf_op jit(solution)/shard_map/ppermute | solution.py:34
  22.0 4.9 %collective-permute-start.3 = (s32[4,1]{1,0:T(4,128)S(1)}, s32[4,1]{1,0:T(4,128)S(1)}, u32[]{:S(2)}, u32[]{:S(2)}) collective-permute-start(s32[4,1]{1,0:T(4,128)S(1)} %get-tuple-element.673), channel_id=1, source_target_pairs={{1,0},{2,1},{3,2},{4,3},{5,4},{6,5},{7,6},{8,7},{9,8},{10,9},{11,1... | collective-permute-start | bytes 56 | tf_op jit(solution)/shard_map/ppermute | solution.py:36
  27.2 53.1 %collective-permute-start.6 = (f32[5,4,1,128]{3,2,1,0:T(1,128)S(1)}, f32[5,4,1,128]{3,2,1,0:T(1,128)S(1)}, u32[]{:S(2)}, u32[]{:S(2)}) collective-permute-start(f32[5,4,1,128]{3,2,1,0:T(1,128)S(1)} %get-tuple-element.664), channel_id=1, source_target_pairs={{0,1},{1,2},{2,3},{3,4},{4,5},{5,6},{6,7},{7,8},{8,9},{9,10},{10,1... | collective-permute-start | bytes 30728 | tf_op jit(solution)/shard_map/ppermute | solution.py:34
  29.1 51.1 %collective-permute-start.7 = (f32[5,4,1,128]{3,2,1,0:T(1,128)S(1)}, f32[5,4,1,128]{3,2,1,0:T(1,128)S(1)}, u32[]{:S(2)}, u32[]{:S(2)}) collective-permute-start(f32[5,4,1,128]{3,2,1,0:T(1,128)S(1)} %get-tuple-element.665), channel_id=1, source_target_pairs={{1,0},{2,1},{3,2},{4,3},{5,4},{6,5},{7,6},{8,7},{9,8},{10,9},{11,1... | collective-permute-start | bytes 30728 | tf_op jit(solution)/shard_map/ppermute | solution.py:36
  126.7 0.8 copy-start.2
  126.8 0.7 copy-start.4
  127.6 2.7 collective-permute-start.8
  129.0 5.3 %collective-permute-start.9 = (f32[5,1,16,128]{3,2,1,0:T(8,128)S(1)}, f32[5,1,16,128]{3,2,1,0:T(8,128)S(1)}, u32[]{:S(2)}, u32[]{:S(2)}) collective-permute-start(f32[5,1,16,128]{3,2,1,0:T(8,128)S(1)} %get-tuple-element.669), channel_id=1, source_target_pairs={{32,0},{64,32},{96,64},{128,96},{160,128},{192,160},{224,192},{33,... | collective-permute-start | bytes 122888 | tf_op jit(solution)/shard_map/ppermute | solution.py:36
  134.3 49.2 %collective-permute-start.10 = (f32[5,4,1,128]{3,2,1,0:T(1,128)S(1)}, f32[5,4,1,128]{3,2,1,0:T(1,128)S(1)}, u32[]{:S(2)}, u32[]{:S(2)}) collective-permute-start(f32[5,4,1,128]{3,2,1,0:T(1,128)S(1)} %get-tuple-element.662), channel_id=1, source_target_pairs={{0,1},{1,2},{2,3},{3,4},{4,5},{5,6},{6,7},{7,8},{8,9},{9,10},{10,1... | collective-permute-start | bytes 30728 | tf_op jit(solution)/shard_map/ppermute | solution.py:34
  139.3 44.2 %collective-permute-start.11 = (f32[5,4,1,128]{3,2,1,0:T(1,128)S(1)}, f32[5,4,1,128]{3,2,1,0:T(1,128)S(1)}, u32[]{:S(2)}, u32[]{:S(2)}) collective-permute-start(f32[5,4,1,128]{3,2,1,0:T(1,128)S(1)} %get-tuple-element.663), channel_id=1, source_target_pairs={{1,0},{2,1},{3,2},{4,3},{5,4},{6,5},{7,6},{8,7},{9,8},{10,9},{11,1... | collective-permute-start | bytes 30728 | tf_op jit(solution)/shard_map/ppermute | solution.py:36
  230.1 2.7 collective-permute-start.12
  231.5 5.3 %collective-permute-start.13 = (f32[5,1,16,128]{3,2,1,0:T(8,128)S(1)}, f32[5,1,16,128]{3,2,1,0:T(8,128)S(1)}, u32[]{:S(2)}, u32[]{:S(2)}) collective-permute-start(f32[5,1,16,128]{3,2,1,0:T(8,128)S(1)} %get-tuple-element.667), channel_id=1, source_target_pairs={{32,0},{64,32},{96,64},{128,96},{160,128},{192,160},{224,192},{33,... | collective-permute-start | bytes 122888 | tf_op jit(solution)/shard_map/ppermute | solution.py:36
  236.8 51.3 %collective-permute-start.14 = (f32[5,4,1,128]{3,2,1,0:T(1,128)S(1)}, f32[5,4,1,128]{3,2,1,0:T(1,128)S(1)}, u32[]{:S(2)}, u32[]{:S(2)}) collective-permute-start(f32[5,4,1,128]{3,2,1,0:T(1,128)S(1)} %get-tuple-element.660), channel_id=1, source_target_pairs={{0,1},{1,2},{2,3},{3,4},{4,5},{5,6},{6,7},{7,8},{8,9},{9,10},{10,1... | collective-permute-start | bytes 30728 | tf_op jit(solution)/shard_map/ppermute | solution.py:34
  241.7 46.5 %collective-permute-start.15 = (f32[5,4,1,128]{3,2,1,0:T(1,128)S(1)}, f32[5,4,1,128]{3,2,1,0:T(1,128)S(1)}, u32[]{:S(2)}, u32[]{:S(2)}) collective-permute-start(f32[5,4,1,128]{3,2,1,0:T(1,128)S(1)} %get-tuple-element.661), channel_id=1, source_target_pairs={{1,0},{2,1},{3,2},{4,3},{5,4},{6,5},{7,6},{8,7},{9,8},{10,9},{11,1... | collective-permute-start | bytes 30728 | tf_op jit(solution)/shard_map/ppermute | solution.py:36
where the time goes:
time: 337 us; the launch traced here: 336 us
  blocking collectives  132 us (39%)
  other arithmetic  127 us (38%)
  starting transfers between devices  41.8 us (12%)
  waiting for transfers between devices  14.2 us (4%)
  loops' own time  12.2 us (4%)
  local copies, waits for them, and re-layouts  5.71 us (2%)
    pmax x12, blocking collectives, by_axis(): return functools.reduce(lax.pmax, axes, array)  132 us
    reduce_sum x24, other arithmetic, one_row(): jnp.sum(scaled * (0.5 * along - jump * dist / (2.0 * sound_speed)), -1)  121 us
    ppermute x8, starting transfers between devices, extended(): lax.ppermute(tail, axis, [(i, (i + 1) % count) for i in range(ends)])  28.5 us
    ppermute x8, waiting for transfers between devices, extended(): lax.ppermute(head, axis, [((i + 1) % count, i) for i in range(ends)])  14.1 us
    ppermute x8, starting transfers between devices, extended(): lax.ppermute(head, axis, [((i + 1) % count, i) for i in range(ends)])  13.3 us
    another operation x3, loops' own time, pair_rates(): result = lax.map(one_row, jnp.arange(rows, dtype=jnp.int32))  12.2 us
  transfers between devices with their start and end apart: 16, of which 4 were waited for; matrix products, arithmetic and copies ran while one was open for 1% of the time, Pallas kernels for 0%

commit v1 on v0

v1 whole, which is shorter than its diff:
```python
import functools
import math

import jax
import jax.numpy as jnp
from jax import lax
from jax.experimental import pallas as pl
from jax.experimental.pallas import tpu as pltpu
from jax.sharding import PartitionSpec as P

ITERS = 3
ROWS = 2
COLS = 16
SLOTS = 128
FIELDS = 8
BLOCK = 16
MESH = pl.DeviceIdType.MESH

courant = 0.2
smoothing = 0.1625
gravity_accel = 9.81
kernel_norm = 7.0 / (4.0 * math.pi * smoothing * smoothing)
grad_coef = -5.0 * kernel_norm / (smoothing * smoothing)
unit = 1.0 / (2.0 * smoothing)
rho_coef = 2.0 * grad_coef * smoothing
vel_coef = -2.0 * grad_coef * 2.0 * smoothing * 5.0
SIDES = tuple((a, b) for a in (-1, 0, 1) for b in (-1, 0, 1) if (a, b) != (0, 0))


def column(row):
    wide = jnp.broadcast_to(row, (COLS, COLS))
    r = lax.broadcasted_iota(jnp.int32, (COLS, COLS), 0)
    c = lax.broadcasted_iota(jnp.int32, (COLS, COLS), 1)
    return jnp.sum(jnp.where(r == c, wide, 0.0), axis=1, keepdims=True)


def pair_terms(own, other, totals):
    xi, yi, vxi, vyi, ppi = own
    xj, yj, vxj, vyj, ppj, wj = other
    ux = xi - xj
    uy = yi - yj
    u2 = ux * ux + uy * uy
    length = u2 * lax.rsqrt(jnp.maximum(u2, 1e-30))
    soft = lax.rsqrt(u2 + 0.0025)
    support = jnp.maximum(1.0 - length, 0.0)
    grad = (support * support) * (support * wj)
    along = (vxi - vxj) * ux + (vyi - vyj) * uy
    force = grad * ((ppi + ppj) - along * soft)
    return (
        totals[0] + grad * (along - (ppi - ppj) * length),
        totals[1] + force * ux,
        totals[2] + force * uy,
    )


def kernel(
    off, den, vel, cnt, wal, o_off, o_den, o_vel,
    field, own_t, rate_t, occ_ref, keep_ref, msg_a, msg_b, slot_a, slot_b,
    halo_send, halo_recv, a_send, a_recv, b_send, b_recv,
):
    gx = lax.axis_index("gx")
    gy = lax.axis_index("gy")
    n_gx = lax.axis_size("gx")
    n_gy = lax.axis_size("gy")
    core = lax.rem(gy, 2)
    plane = lax.div(gy, 2)
    n_plane = n_gy // 2

    def side(a, b):
        return {"gx": lax.rem(gx + a + n_gx, n_gx), "gy": lax.rem(gy + b + n_gy, n_gy)}

    def peer_a(k):
        return {"gx": lax.rem(gx + k // 2, n_gx), "gy": plane * 2 + (lax.rem(core + 1, 2) if k % 2 else core)}

    def peer_b(k):
        return {"gx": gx, "gy": lax.rem(plane + k, n_plane) * 2 + core}

    peers_a = [peer_a(k) for k in range(1, 2 * n_gx)]
    peers_b = [peer_b(k) for k in range(1, n_plane)]
    sides = [side(a, b) for a, b in SIDES]

    barrier = pltpu.get_barrier_semaphore()
    for target in peers_a + peers_b + sides:
        pl.semaphore_signal(barrier, inc=1, device_id=target, device_id_type=MESH)

    lane = lax.broadcasted_iota(jnp.int32, (COLS, SLOTS), 1)
    for a in range(ROWS):
        occ = (lane.astype(jnp.float32) < column(cnt[a : a + 1, :].astype(jnp.float32))).astype(jnp.float32)
        keep = jnp.broadcast_to(column(1.0 - wal[a : a + 1, :].astype(jnp.float32)), (COLS, SLOTS))
        occ_ref[a] = occ
        keep_ref[a] = keep
        for c in range(2):
            o_off[c, a] = off[c, a]
            o_vel[c, a] = vel[c, a] * keep
        o_den[a] = den[a]

    def publish(s):
        best = jnp.zeros((COLS, SLOTS), jnp.float32)
        for a in range(ROWS):
            occ = occ_ref[a]
            rho = o_den[a]
            vx = o_vel[0, a]
            vy = o_vel[1, a]
            best = jnp.maximum(best, occ * (vx * vx + vy * vy))
            rows = [
                o_off[0, a] * unit,
                o_off[1, a] * unit,
                vx,
                vy,
                10.0 * (rho - 1.0),
                occ / (64.0 * (rho + 1.0 - occ)),
                occ,
                jnp.zeros_like(occ),
            ]
            for f in range(FIELDS):
                for b in range(COLS):
                    field[s, a + 1, b + 1, f : f + 1, :] = rows[f][b : b + 1]
            own_t[a] = jnp.concatenate(rows, 0).T
        msg_a[s] = jnp.broadcast_to(jnp.max(best, keepdims=True).reshape(1, 1), (1, SLOTS))

    def halo(s):
        copies = []
        for k, (a, b) in enumerate(SIDES):
            src_r = pl.ds(1, 2) if a == 0 else (1 if a < 0 else 2)
            dst_r = pl.ds(1, 2) if a == 0 else (3 if a < 0 else 0)
            src_c = pl.ds(1, COLS) if b == 0 else (1 if b < 0 else COLS)
            dst_c = pl.ds(1, COLS) if b == 0 else (COLS + 1 if b < 0 else 0)
            copies.append(
                pltpu.make_async_remote_copy(
                    src_ref=field.at[s, src_r, src_c],
                    dst_ref=field.at[s, dst_r, dst_c],
                    send_sem=halo_send.at[s, k],
                    recv_sem=halo_recv.at[s, k],
                    device_id=sides[k],
                    device_id_type=MESH,
                )
            )
        return copies

    def spread(s, peers, msg, slots, me, send, recv):
        slots[s, me] = msg[s]
        for target in peers:
            pltpu.make_async_remote_copy(
                src_ref=msg.at[s], dst_ref=slots.at[s, me], send_sem=send.at[s], recv_sem=recv.at[s],
                device_id=target, device_id_type=MESH,
            ).start()

    def gathered(s, peers, slots, send, recv):
        n = len(peers)
        whole = slots.at[s, pl.ds(0, n)]
        return pltpu.make_async_remote_copy(
            src_ref=whole, dst_ref=whole, send_sem=send.at[s], recv_sem=recv.at[s],
            device_id=peers[0], device_id_type=MESH,
        )

    def clear_outside(s):
        zeros_row = jnp.zeros((COLS + 2, FIELDS, SLOTS), jnp.float32)
        zeros_col = jnp.zeros((ROWS + 2, 1, FIELDS, SLOTS), jnp.float32)

        @pl.when(gx == 0)
        def _():
            field[s, 0] = zeros_row

        @pl.when(gx == n_gx - 1)
        def _():
            field[s, ROWS + 1] = zeros_row

        @pl.when(gy == 0)
        def _():
            field[s, :, 0:1] = zeros_col

        @pl.when(gy == n_gy - 1)
        def _():
            field[s, :, COLS + 1 : COLS + 2] = zeros_col

    lanes = lax.broadcasted_iota(jnp.int32, (BLOCK, SLOTS), 1)
    zeros = jnp.zeros((BLOCK, SLOTS), jnp.float32)

    def dense(s):
        def tile(t, carry):
            a = lax.div(t, SLOTS // BLOCK)
            i0 = pl.multiple_of(lax.rem(t, SLOTS // BLOCK) * BLOCK, BLOCK)
            mine = own_t[a, pl.ds(i0, BLOCK), :]

            def cell(b, rates):
                turned = pltpu.roll(mine, lax.rem(SLOTS - b, SLOTS), 1)
                own = [jnp.broadcast_to(turned[:, COLS * f : COLS * f + 1], (BLOCK, SLOTS)) for f in range(5)]
                totals = (zeros, zeros, zeros)
                for da in range(3):
                    for db in range(3):
                        rows = [field[s, a + da, b + db, f : f + 1, :] for f in range(6)]
                        rows[0] = rows[0] + (da - 1) * unit
                        rows[1] = rows[1] + (db - 1) * unit
                        totals = pair_terms(own, rows, totals)
                for f in range(3):
                    rates = jnp.where(lanes == f * COLS + b, jnp.sum(totals[f], 1, keepdims=True), rates)
                return rates

            rate_t[a, pl.ds(i0, BLOCK), :] = lax.fori_loop(0, COLS, cell, zeros)
            return carry

        lax.fori_loop(0, ROWS * SLOTS // BLOCK, tile, 0)

    def update(s, step):
        for a in range(ROWS):
            rates = rate_t[a].T
            occ = occ_ref[a]
            keep = keep_ref[a]
            rho = o_den[a]
            gain = step * occ
            scale = vel_coef / (rho + 1.0 - occ)
            o_den[a] = rho + gain * (rho_coef * rho * rates[0:COLS])
            vx = (o_vel[0, a] + gain * (scale * rates[COLS : 2 * COLS])) * keep
            vy = (o_vel[1, a] + gain * (scale * rates[2 * COLS : 3 * COLS] - gravity_accel)) * keep
            o_vel[0, a] = vx
            o_vel[1, a] = vy
            o_off[0, a] = o_off[0, a] + gain * vx
            o_off[1, a] = o_off[1, a] + gain * vy

    me_a = gx * 2 + core
    me_b = plane
    for s in range(ITERS):
        publish(s)
        if s == 0:
            pl.semaphore_wait(barrier, len(peers_a) + len(peers_b) + len(sides))
        copies = halo(s)
        for copy in copies:
            copy.start()
        spread(s, peers_a, msg_a, slot_a, me_a, a_send, a_recv)
        for copy in copies:
            copy.wait_recv()
        clear_outside(s)
        gathered(s, peers_a, slot_a, a_send, a_recv).wait_recv()
        msg_b[s] = jnp.max(slot_a[s], axis=0)
        spread(s, peers_b, msg_b, slot_b, me_b, b_send, b_recv)
        dense(s)
        gathered(s, peers_b, slot_b, b_send, b_recv).wait_recv()
        top = 10.0 + jnp.sqrt(jnp.max(slot_b[s], axis=0))
        update(s, courant * smoothing / top)
        for copy in copies:
            copy.wait_send()
        gathered(s, peers_a, slot_a, a_send, a_recv).wait_send()
        gathered(s, peers_b, slot_b, b_send, b_recv).wait_send()


def shards(n_gx, n_gy, offsets, density, velocity, counts, walls):
    shape = jax.ShapeDtypeStruct
    dma = pltpu.SemaphoreType.DMA
    f32 = jnp.float32
    n_a, n_b = 2 * n_gx, n_gy // 2
    return pl.pallas_call(
        kernel,
        out_shape=(shape(offsets.shape, f32), shape(density.shape, f32), shape(velocity.shape, f32)),
        in_specs=[pl.BlockSpec(memory_space=pltpu.VMEM)] * 5,
        out_specs=tuple(pl.BlockSpec(memory_space=pltpu.VMEM) for _ in range(3)),
        scratch_shapes=[
            pltpu.VMEM((ITERS, ROWS + 2, COLS + 2, FIELDS, SLOTS), f32),
            pltpu.VMEM((ROWS, SLOTS, SLOTS), f32),
            pltpu.VMEM((ROWS, SLOTS, SLOTS), f32),
            pltpu.VMEM((ROWS, COLS, SLOTS), f32),
            pltpu.VMEM((ROWS, COLS, SLOTS), f32),
            pltpu.VMEM((ITERS, 1, SLOTS), f32),
            pltpu.VMEM((ITERS, 1, SLOTS), f32),
            pltpu.VMEM((ITERS, n_a, 1, SLOTS), f32),
            pltpu.VMEM((ITERS, n_b, 1, SLOTS), f32),
            dma((ITERS, 8)),
            dma((ITERS, 8)),
            dma((ITERS,)),
            dma((ITERS,)),
            dma((ITERS,)),
            dma((ITERS,)),
        ],
        compiler_params=pltpu.CompilerParams(collective_id=0, has_side_effects=True),
    )(offsets, density, velocity, counts, walls)


def solution(mesh):
    fields = P(None, "gx", "gy", None)
    cells = P("gx", "gy")
    return jax.shard_map(
        functools.partial(shards, mesh.shape["gx"], mesh.shape["gy"]),
        mesh=mesh,
        in_specs=(fields, P("gx", "gy", None), fields, cells, cells),
        out_specs=(fields, P("gx", "gy", None), fields),
        check_vma=False,
    )
```

time: 337 us -> 265 us (0.79)
  Pallas kernels: 0 us -> 262 us
  blocking collectives: 132 us -> 0 us
  other arithmetic: 127 us -> 0 us
  starting transfers between devices: 41.8 us -> 0 us
  waiting for transfers between devices: 14.2 us -> 0 us
  loops' own time: 12.2 us -> 0 us
    pallas_call x0 -> x1, Pallas kernels: none -> 262 us  [shards(): pl.pallas_call(kernel, out_shape=(shape(offsets.shape, f32), shape(densit...]
    pmax x12 -> x0, blocking collectives: 132 us -> none  [by_axis(): return functools.reduce(lax.pmax, axes, array)]
    reduce_sum x24 -> x0, other arithmetic: 121 us -> none  [one_row(): jnp.sum(scaled * (0.5 * along - jump * dist / (2.0 * sound_speed)), -1)]
    ppermute x16 -> x0, starting transfers between devices: 41.8 us -> none  [the longest x8 28.5 us: extended(): lax.ppermute(tail, axis, [(i, (i + 1) % count) for i in range(ends)])]
    ppermute x16 -> x0, waiting for transfers between devices: 14.2 us -> none  [the longest x8 14.1 us: extended(): lax.ppermute(head, axis, [((i + 1) % count, i) for i in range(ends)])]
    another operation x3 -> x0, loops' own time: 12.2 us -> none  [pair_rates(): result = lax.map(one_row, jnp.arange(rows, dtype=jnp.int32))]
    dynamic_slice x6 -> x0, local copies, waits for them, and re-layouts: 3.53 us -> none  [pair_rates(): result = lax.map(one_row, jnp.arange(rows, dtype=jnp.int32))]
  transfers between devices with their start and end apart: 16 -> 0, of which waited for: 4 -> 0; matrix products, arithmetic and copies ran while one was open for 1% -> 0% of each run, Pallas kernels for 0% -> 0%
where the time goes in v1:
time: 265 us
  Pallas kernels  262 us (99%)
    pallas_call x1, Pallas kernels, shards(): pl.pallas_call(kernel, out_shape=(shape(offsets.shape, f32), shape(densit...  262 us

profile of v1, /device:TPU:1, one launch (start us, length us, event | category | flops | bytes accessed | tf_op | source)
XLA Modules:
  0.0 265.0 jit_solution(14762678175365665827)
XLA Ops:
  0.6 261.7 %shard_map.76 = (f32[2,2,16,128]{3,2,1,0:T(8,128)}, f32[2,16,128]{2,1,0:T(8,128)}, f32[2,2,16,128]{3,2,1,0:T(8,128)}) custom-call(f32[2,2,16,128]{3,2,1,0:T(8,128)} %off.1, f32[2,16,128]{2,1,0:T(8,128)} %den.1, f32[2,2,16,128]{3,2,1,0:T(8,128)} %vel.1, s32[2,16]{1,0:T(2,128)} %cnt.1, s32[2,16]{1,0:T(2,128)} %wal.1), custom_call_target="tpu_custom_call" | custom-call | tf_op jit(solution)/shard_map/pallas_call | solution.py:251
  262.4 0.0 copy-start.1
  262.4 0.0 copy-start
  262.4 1.4 copy.11
  263.8 0.0 copy-done.1
  263.8 0.6 copy.12
  264.4 0.0 copy-done
  264.4 0.6 copy.13
Async XLA Ops:
  262.4 1.4 copy-start.1
  262.4 2.0 copy-start

commit v2 on v1

--- a/solution.py
+++ b/solution.py
@@ -14,6 +14,10 @@
 SLOTS = 128
 FIELDS = 8
 BLOCK = 16
+OWN_FIELDS = 5
+CELLS = ROWS * COLS
+PAIRS = CELLS // 2
+RING = 2
 MESH = pl.DeviceIdType.MESH
 
 courant = 0.2
@@ -24,6 +28,8 @@
 unit = 1.0 / (2.0 * smoothing)
 rho_coef = 2.0 * grad_coef * smoothing
 vel_coef = -2.0 * grad_coef * 2.0 * smoothing * 5.0
+longest = 2.0 * courant * smoothing / 10.0
+margin = 0.01
 SIDES = tuple((a, b) for a in (-1, 0, 1) for b in (-1, 0, 1) if (a, b) != (0, 0))
 
 
@@ -53,11 +59,24 @@
     )
 
 
+def pieces(x):
+    high = x.astype(jnp.bfloat16).astype(jnp.float32)
+    rest = x - high
+    middle = rest.astype(jnp.bfloat16).astype(jnp.float32)
+    return high, middle, rest - middle
+
+
 def kernel(
-    off, den, vel, cnt, wal, o_off, o_den, o_vel,
-    field, own_t, rate_t, occ_ref, keep_ref, msg_a, msg_b, slot_a, slot_b,
-    halo_send, halo_recv, a_send, a_recv, b_send, b_recv,
+    ring, off, den, vel, cnt, wal, o_off, o_den, o_vel, o_flag,
+    field, rate_t, occ_ref, keep_ref, msg_a, msg_b, slot_a, slot_b,
+    halo_send, halo_recv, a_send, a_recv, b_send, b_recv, *extra,
 ):
+    f32 = jnp.float32
+    if ring:
+        own_p, pick, bc0, bc1, acc0, acc1, ring0, ring1, code, natural, ranks, box_lo, box_hi, bad = extra
+        bcs, accs, rings = (bc0, bc1), (acc0, acc1), (ring0, ring1)
+    else:
+        (own_t,) = extra
     gx = lax.axis_index("gx")
     gy = lax.axis_index("gy")
     n_gx = lax.axis_size("gx")
@@ -84,29 +103,46 @@
         pl.semaphore_signal(barrier, inc=1, device_id=target, device_id_type=MESH)
 
     lane = lax.broadcasted_iota(jnp.int32, (COLS, SLOTS), 1)
+    lane_row = lax.broadcasted_iota(jnp.int32, (1, SLOTS), 1)
     for a in range(ROWS):
-        occ = (lane.astype(jnp.float32) < column(cnt[a : a + 1, :].astype(jnp.float32))).astype(jnp.float32)
-        keep = jnp.broadcast_to(column(1.0 - wal[a : a + 1, :].astype(jnp.float32)), (COLS, SLOTS))
+        occ = (lane.astype(f32) < column(cnt[a : a + 1, :].astype(f32))).astype(f32)
+        keep = jnp.broadcast_to(column(1.0 - wal[a : a + 1, :].astype(f32)), (COLS, SLOTS))
         occ_ref[a] = occ
         keep_ref[a] = keep
         for c in range(2):
             o_off[c, a] = off[c, a]
             o_vel[c, a] = vel[c, a] * keep
         o_den[a] = den[a]
+    rate_t[...] = jnp.zeros_like(rate_t)
+    if ring:
+        bad[...] = jnp.zeros_like(bad)
+        r = lax.broadcasted_iota(jnp.int32, pick.shape, 0)
+        c = lax.broadcasted_iota(jnp.int32, pick.shape, 1)
+        group = r // COLS
+        hit = (group % OWN_FIELDS == c // SLOTS) & (group < 3 * OWN_FIELDS)
+        pick[...] = jnp.where(hit, 1.0, 0.0).astype(jnp.bfloat16)
+
+    def fastest(s):
+        best = jnp.zeros((COLS, SLOTS), f32)
+        for a in range(ROWS):
+            vx = o_vel[0, a]
+            vy = o_vel[1, a]
+            best = jnp.maximum(best, occ_ref[a] * (vx * vx + vy * vy))
+        best = jnp.max(best, keepdims=True).reshape(1, 1)
+        if ring:
+            msg_a[s] = jnp.where(lane_row < SLOTS // 2, best, jnp.max(bad[...], keepdims=True).reshape(1, 1))
+        else:
+            msg_a[s] = jnp.broadcast_to(best, (1, SLOTS))
 
     def publish(s):
-        best = jnp.zeros((COLS, SLOTS), jnp.float32)
         for a in range(ROWS):
             occ = occ_ref[a]
             rho = o_den[a]
-            vx = o_vel[0, a]
-            vy = o_vel[1, a]
-            best = jnp.maximum(best, occ * (vx * vx + vy * vy))
             rows = [
                 o_off[0, a] * unit,
                 o_off[1, a] * unit,
-                vx,
-                vy,
+                o_vel[0, a],
+                o_vel[1, a],
                 10.0 * (rho - 1.0),
                 occ / (64.0 * (rho + 1.0 - occ)),
                 occ,
@@ -115,8 +151,19 @@
             for f in range(FIELDS):
                 for b in range(COLS):
                     field[s, a + 1, b + 1, f : f + 1, :] = rows[f][b : b + 1]
-            own_t[a] = jnp.concatenate(rows, 0).T
-        msg_a[s] = jnp.broadcast_to(jnp.max(best, keepdims=True).reshape(1, 1), (1, SLOTS))
+            if not ring:
+                own_t[a] = jnp.concatenate(rows, 0).T
+
+    def turn():
+        for a in range(ROWS):
+            rows = [
+                o_off[0, a] * unit, o_off[1, a] * unit, o_vel[0, a], o_vel[1, a], 10.0 * (o_den[a] - 1.0),
+            ]
+            parts = [pieces(x) for x in rows]
+            flat = [p[n] for n in range(3) for p in parts] + [jnp.zeros((COLS, SLOTS), f32)]
+            for n in range(2):
+                half = jnp.concatenate(flat[8 * n : 8 * n + 8], 0)
+                own_p[a, :, n * SLOTS : (n + 1) * SLOTS] = half.T.astype(jnp.bfloat16)
 
     def halo(s):
         copies = []
@@ -154,8 +201,8 @@
         )
 
     def clear_outside(s):
-        zeros_row = jnp.zeros((COLS + 2, FIELDS, SLOTS), jnp.float32)
-        zeros_col = jnp.zeros((ROWS + 2, 1, FIELDS, SLOTS), jnp.float32)
+        zeros_row = jnp.zeros((COLS + 2, FIELDS, SLOTS), f32)
+        zeros_col = jnp.zeros((ROWS + 2, 1, FIELDS, SLOTS), f32)
 
         @pl.when(gx == 0)
         def _():
@@ -174,7 +221,7 @@
             field[s, :, COLS + 1 : COLS + 2] = zeros_col
 
     lanes = lax.broadcasted_iota(jnp.int32, (BLOCK, SLOTS), 1)
-    zeros = jnp.zeros((BLOCK, SLOTS), jnp.float32)
+    zeros = jnp.zeros((BLOCK, SLOTS), f32)
 
     def dense(s):
         def tile(t, carry):
@@ -200,6 +247,151 @@
             return carry
 
         lax.fori_loop(0, ROWS * SLOTS // BLOCK, tile, 0)
+
+    def boxes():
+        for a in range(ROWS):
+            for d in range(2):
+                x = o_off[d, a] * unit
+                way = o_vel[d, a] * (longest * unit)
+                box_lo[d, a] = x + jnp.minimum(way, 0.0) - margin * unit
+                box_hi[d, a] = x + jnp.maximum(way, 0.0) + margin * unit
+
+    def check():
+        for a in range(ROWS):
+            inside = occ_ref[a] < 0.5
+            both = None
+            for d in range(2):
+                x = o_off[d, a] * unit
+                within = (x >= box_lo[d, a]) & (x <= box_hi[d, a])
+                both = within if both is None else both & within
+            bad[...] = jnp.maximum(bad[...], jnp.where(inside | both, 0.0, 1.0))
+
+    def lists():
+        def copy_row(t, carry):
+            r = lax.div(t, COLS + 2)
+            c = lax.rem(t, COLS + 2)
+            for n, f in enumerate((0, 1, 2, 3, 6)):
+                natural[n, r, pl.ds(c, 1), :] = field[0, r, c, f : f + 1, :]
+            return carry
+
+        lax.fori_loop(0, (ROWS + 2) * (COLS + 2), copy_row, 0)
+        reach = 1.0001
+        masks = []
+        for k, (da, db) in enumerate(SIDES):
+            for a in range(ROWS):
+                there = [natural[n, a + 1 + da, 1 + db : 1 + db + COLS, :] for n in range(5)]
+                near = there[4] > 0.5
+                for d, shift in ((0, da), (1, db)):
+                    occ = occ_ref[a] > 0.5
+                    low = jnp.min(jnp.where(occ, box_lo[d, a], 1e30), axis=1, keepdims=True) - reach
+                    high = jnp.max(jnp.where(occ, box_hi[d, a], -1e30), axis=1, keepdims=True) + reach
+                    x = there[d] + shift * unit
+                    way = there[2 + d] * (longest * unit)
+                    near = near & (x + jnp.maximum(way, 0.0) + margin * unit > low)
+                    near = near & (x + jnp.minimum(way, 0.0) - margin * unit < high)
+                masks.append(jnp.where(near, 1.0, 0.0))
+        r = lax.broadcasted_iota(jnp.int32, (SLOTS, SLOTS), 0)
+        c = lax.broadcasted_iota(jnp.int32, (SLOTS, SLOTS), 1)
+        upper = jnp.where(r <= c, 1.0, 0.0).astype(jnp.bfloat16)
+        stacked = jnp.concatenate(masks, 0).astype(jnp.bfloat16)
+        ranks[...] = jnp.dot(stacked, upper, preferred_element_type=f32).astype(jnp.int32)
+        where_to = lax.broadcasted_iota(jnp.int32, (8, SLOTS), 1)
+        for g in range(CELLS // 8):
+            base = jnp.zeros((8, 1), jnp.int32)
+            for k in range(8):
+                table = ranks[(k * CELLS + 8 * g) : (k * CELLS + 8 * g + 8), :]
+                count = table[:, SLOTS - 1 : SLOTS]
+                for t in range(RING):
+                    rank = where_to + (SLOTS * t + 1) - base
+                    spot = jnp.zeros((8, SLOTS), jnp.int32)
+                    for bit in (64, 32, 16, 8, 4, 2, 1):
+                        probe = jnp.take_along_axis(table, spot + (bit - 1), axis=1)
+                        spot = jnp.where(probe < rank, spot + bit, spot)
+                    code[t, k, 8 * g : 8 * g + 8, :] = jnp.where((rank >= 1) & (rank <= count), spot, -1)
+                base = base + count
+            over = jnp.where(base > RING * SLOTS, 1.0, 0.0)
+            bad[0:8, :] = jnp.maximum(bad[0:8, :], jnp.broadcast_to(over, (8, SLOTS)))
+
+    field_row = lax.broadcasted_iota(jnp.int32, (FIELDS, SLOTS), 0)
+
+    def broadcast_own(c, dst):
+        a = lax.div(c, COLS)
+        b = lax.rem(c, COLS)
+        mine = own_p[a]
+        at = lax.broadcasted_iota(jnp.int32, mine.shape, 1) % COLS
+        mine = jnp.where(at == b, mine.astype(f32), 0.0).astype(jnp.bfloat16)
+        wide = jnp.dot(mine, pick[...], preferred_element_type=f32)
+        for f in range(OWN_FIELDS):
+            dst[f] = wide[:, f * SLOTS : (f + 1) * SLOTS]
+
+    def sweep(bc, acc, tiles, first):
+        for i0 in range(0, SLOTS, BLOCK):
+            here = pl.ds(i0, BLOCK)
+            own = [bc[f, here, :] for f in range(OWN_FIELDS)]
+            totals = (zeros, zeros, zeros) if first else tuple(acc[f, here, :] for f in range(3))
+            for rows in tiles:
+                totals = pair_terms(own, rows, totals)
+            for f in range(3):
+                acc[f, here, :] = totals[f]
+
+    def own_pass(s):
+        broadcast_own(0, bc0.at[0])
+
+        def two(u, carry):
+            for n in range(2):
+                c = 2 * u + n
+                a = lax.div(c, COLS)
+                b = lax.rem(c, COLS)
+                later = jnp.minimum(c + 1, CELLS - 1)
+                broadcast_own(later, bcs[1 - n].at[u + n])
+                rows = [field[s, a + 1, b + 1, f : f + 1, :] for f in range(6)]
+                sweep(bcs[n].at[u], accs[n].at[u], [rows], True)
+            return carry
+
+        lax.fori_loop(0, PAIRS, two, 0)
+
+    def pack(s, c, dst):
+        a = lax.div(c, COLS)
+        b = lax.rem(c, COLS)
+        for t in range(RING):
+            packed = jnp.zeros((FIELDS, SLOTS), f32)
+            for k, (da, db) in enumerate(SIDES):
+                take = jnp.broadcast_to(code[t, k, pl.ds(c, 1), :], (FIELDS, SLOTS))
+                moved = jnp.take_along_axis(field[s, a + 1 + da, b + 1 + db], take & (SLOTS - 1), axis=1)
+                shift = jnp.where(field_row == 0, da * unit, jnp.where(field_row == 1, db * unit, 0.0))
+                packed = jnp.where(take >= 0, moved + shift, packed)
+            dst[t] = packed
+
+    def collect(c, acc, valid):
+        a = lax.div(c, COLS)
+        b = lax.rem(c, COLS)
+        if valid is not None:
+            b = jnp.where(valid, b, -4 * SLOTS)
+        for i0 in range(0, SLOTS, BLOCK):
+            here = pl.ds(i0, BLOCK)
+            rates = rate_t[a, here, :]
+            for f in range(3):
+                rates = jnp.where(lanes == f * COLS + b, jnp.sum(acc[f, here, :], 1, keepdims=True), rates)
+            rate_t[a, here, :] = rates
+
+    def ring_pass(s):
+        for n in range(2):
+            pack(s, n, rings[n].at[0])
+
+        def two(u, carry):
+            for n in range(2):
+                c = 2 * u + n
+                if n == 0:
+                    collect(jnp.maximum(c - 1, 0), acc1.at[jnp.maximum(u - 1, 0)], c > 0)
+                else:
+                    collect(c - 1, acc0.at[u], None)
+                tiles = [[rings[n][u, t, f : f + 1, :] for f in range(6)] for t in range(RING)]
+                sweep(bcs[n].at[u], accs[n].at[u], tiles, False)
+                pack(s, jnp.minimum(c + 2, CELLS - 1), rings[n].at[u + 1])
+            return carry
+
+        lax.fori_loop(0, PAIRS, two, 0)
+        collect(CELLS - 1, acc1.at[PAIRS - 1], None)
 
     def update(s, step):
         for a in range(ROWS):
@@ -220,42 +412,80 @@
     me_a = gx * 2 + core
     me_b = plane
     for s in range(ITERS):
-        publish(s)
+        fastest(s)
         if s == 0:
             pl.semaphore_wait(barrier, len(peers_a) + len(peers_b) + len(sides))
+        spread(s, peers_a, msg_a, slot_a, me_a, a_send, a_recv)
+        publish(s)
         copies = halo(s)
         for copy in copies:
             copy.start()
-        spread(s, peers_a, msg_a, slot_a, me_a, a_send, a_recv)
+        if ring:
+            if s == 0:
+                boxes()
+            turn()
+            own_pass(s)
+        gathered(s, peers_a, slot_a, a_send, a_recv).wait_recv()
+        msg_b[s] = jnp.max(slot_a[s], axis=0)
+        spread(s, peers_b, msg_b, slot_b, me_b, b_send, b_recv)
         for copy in copies:
             copy.wait_recv()
         clear_outside(s)
-        gathered(s, peers_a, slot_a, a_send, a_recv).wait_recv()
-        msg_b[s] = jnp.max(slot_a[s], axis=0)
-        spread(s, peers_b, msg_b, slot_b, me_b, b_send, b_recv)
-        dense(s)
+        if ring:
+            if s == 0:
+                lists()
+            ring_pass(s)
+        else:
+            dense(s)
         gathered(s, peers_b, slot_b, b_send, b_recv).wait_recv()
-        top = 10.0 + jnp.sqrt(jnp.max(slot_b[s], axis=0))
+        result = jnp.max(slot_b[s], axis=0)
+        top = 10.0 + jnp.sqrt(result[:, 0:1])
         update(s, courant * smoothing / top)
+        if ring and s < ITERS - 1:
+            check()
         for copy in copies:
             copy.wait_send()
         gathered(s, peers_a, slot_a, a_send, a_recv).wait_send()
         gathered(s, peers_b, slot_b, b_send, b_recv).wait_send()
-
-
-def shards(n_gx, n_gy, offsets, density, velocity, counts, walls):
+    o_flag[...] = result
+
+
+def substeps(ring, n_gx, n_gy, offsets, density, velocity, counts, walls):
     shape = jax.ShapeDtypeStruct
     dma = pltpu.SemaphoreType.DMA
     f32 = jnp.float32
     n_a, n_b = 2 * n_gx, n_gy // 2
+    if ring:
+        extra = [
+            pltpu.VMEM((ROWS, SLOTS, 2 * SLOTS), jnp.bfloat16),
+            pltpu.VMEM((2 * SLOTS, OWN_FIELDS * SLOTS), jnp.bfloat16),
+            pltpu.VMEM((PAIRS + 1, OWN_FIELDS, SLOTS, SLOTS), f32),
+            pltpu.VMEM((PAIRS + 1, OWN_FIELDS, SLOTS, SLOTS), f32),
+            pltpu.VMEM((PAIRS, 3, SLOTS, SLOTS), f32),
+            pltpu.VMEM((PAIRS, 3, SLOTS, SLOTS), f32),
+            pltpu.VMEM((PAIRS + 1, RING, FIELDS, SLOTS), f32),
+            pltpu.VMEM((PAIRS + 1, RING, FIELDS, SLOTS), f32),
+            pltpu.VMEM((RING, 8, CELLS, SLOTS), jnp.int32),
+            pltpu.VMEM((5, ROWS + 2, 24, SLOTS), f32),
+            pltpu.VMEM((8 * CELLS, SLOTS), jnp.int32),
+            pltpu.VMEM((2, ROWS, COLS, SLOTS), f32),
+            pltpu.VMEM((2, ROWS, COLS, SLOTS), f32),
+            pltpu.VMEM((COLS, SLOTS), f32),
+        ]
+    else:
+        extra = [pltpu.VMEM((ROWS, SLOTS, SLOTS), f32)]
     return pl.pallas_call(
-        kernel,
-        out_shape=(shape(offsets.shape, f32), shape(density.shape, f32), shape(velocity.shape, f32)),
+        functools.partial(kernel, ring),
+        out_shape=(
+            shape(offsets.shape, f32),
+            shape(density.shape, f32),
+            shape(velocity.shape, f32),
+            shape((1, SLOTS), f32),
+        ),
         in_specs=[pl.BlockSpec(memory_space=pltpu.VMEM)] * 5,
-        out_specs=tuple(pl.BlockSpec(memory_space=pltpu.VMEM) for _ in range(3)),
+        out_specs=tuple(pl.BlockSpec(memory_space=pltpu.VMEM) for _ in range(4)),
         scratch_shapes=[
             pltpu.VMEM((ITERS, ROWS + 2, COLS + 2, FIELDS, SLOTS), f32),
-            pltpu.VMEM((ROWS, SLOTS, SLOTS), f32),
             pltpu.VMEM((ROWS, SLOTS, SLOTS), f32),
             pltpu.VMEM((ROWS, COLS, SLOTS), f32),
             pltpu.VMEM((ROWS, COLS, SLOTS), f32),
@@ -269,9 +499,19 @@
             dma((ITERS,)),
             dma((ITERS,)),
             dma((ITERS,)),
-        ],
-        compiler_params=pltpu.CompilerParams(collective_id=0, has_side_effects=True),
+        ]
+        + extra,
+        compiler_params=pltpu.CompilerParams(collective_id=0 if ring else 1, has_side_effects=True),
     )(offsets, density, velocity, counts, walls)
+
+
+def shards(n_gx, n_gy, *args):
+    *fast, flag = substeps(True, n_gx, n_gy, *args)
+    return lax.cond(
+        flag[0, SLOTS - 1] > 0.0,
+        lambda: tuple(substeps(False, n_gx, n_gy, *args)[:3]),
+        lambda: tuple(fast),
+    )
 
 
 def solution(mesh):

time: 265 us -> 60.8 us (0.23)
  Pallas kernels: 262 us -> 54.9 us
    pallas_call x1, Pallas kernels: 262 us -> 54.9 us  [substeps(): pl.pallas_call(functools.partial(kernel, ring), out_shape=(shape(offsets....]
where the time goes in v2:
time: 60.8 us; the launch traced here: 60.6 us
  Pallas kernels  54.9 us (90%)
  local copies, waits for them, and re-layouts  4.36 us (7%)
  between operations  1.34 us (2%)
    pallas_call x1, Pallas kernels, substeps(): pl.pallas_call(functools.partial(kernel, ring), out_shape=(shape(offsets....  54.9 us
    unnamed x15, local copies, waits for them, and re-layouts  3.78 us

profile of v2, /device:TPU:1, one launch (start us, length us, event | category | flops | bytes accessed | tf_op | source)
XLA Modules:
  0.0 60.6 jit_solution(13501300207489867188)
XLA Ops:
  0.6 0.0 copy-start.3
  0.6 0.7 %copy-done.3 = s32[2,16]{1,0:T(2,128)S(1)} copy-done((s32[2,16]{1,0:T(2,128)S(1)}, s32[2,16]{1,0:T(2,128)}, u32[]{:S(2)}) %copy-start.3) | copy-done | bytes 152
  1.3 0.0 copy-start
  1.3 0.0 copy-start.1
  1.3 0.0 copy-start.2
  1.3 54.9 %shard_map.82 = (f32[2,2,16,128]{3,2,1,0:T(8,128)S(1)}, f32[2,16,128]{2,1,0:T(8,128)S(1)}, f32[2,2,16,128]{3,2,1,0:T(8,128)S(1)}, f32[1,128]{1,0:T(1,128)}) custom-call(f32[2,2,16,128]{3,2,1,0:T(8,128)} %off.1, f32[2,16,128]{2,1,0:T(8,128)} %den.1, f32[2,2,16,128]{3,2,1,0:T(8,128)} %vel.1, s32[2,16]{1,0:T(2,128)S(1)} %copy-done.3, s32[2,16]{1,0:T(2,128)} %wal.1), custom_call_target="tpu_custom_call" | custom-call | tf_op jit(solution)/shard_map/pallas_call | solution.py:477
  56.2 0.0 copy-start.5
  56.2 0.6 %copy-done.5 = f32[1,128]{1,0:T(1,128)S(1)} copy-done((f32[1,128]{1,0:T(1,128)S(1)}, f32[1,128]{1,0:T(1,128)}, u32[]{:S(2)}) %copy-start.5) | copy-done | bytes 536
  56.8 0.6 slice.3
  58.1 0.0 copy-start.4
  58.1 0.0 copy-done
  58.1 0.0 copy-done.1
  58.1 0.0 copy-done.2
  58.1 0.6 %copy-done.4 = s32[2,16]{1,0:T(2,128)S(1)} copy-done((s32[2,16]{1,0:T(2,128)S(1)}, s32[2,16]{1,0:T(2,128)}, u32[]{:S(2)}) %copy-start.4) | copy-done | bytes 152
  58.8 0.6 %copy.23 = f32[2,2,16,128]{3,2,1,0:T(8,128)} copy(f32[2,2,16,128]{3,2,1,0:T(8,128)S(1)} %get-tuple-element.50) | data formatting | bytes 65536
  59.4 0.6 copy.24
  60.0 0.6 %copy.25 = f32[2,2,16,128]{3,2,1,0:T(8,128)} copy(f32[2,2,16,128]{3,2,1,0:T(8,128)S(1)} %get-tuple-element.52) | data formatting | bytes 65536
  (1 shorter events, 0.0 us)
Async XLA Ops:
  0.6 0.7 %copy-start.3 = (s32[2,16]{1,0:T(2,128)S(1)}, s32[2,16]{1,0:T(2,128)}, u32[]{:S(2)}) copy-start(s32[2,16]{1,0:T(2,128)} %cnt.1) | copy-start | bytes 388
  1.3 56.8 %copy-start = (f32[2,2,16,128]{3,2,1,0:T(8,128)S(1)}, f32[2,2,16,128]{3,2,1,0:T(8,128)}, u32[]{:S(2)}) copy-start(f32[2,2,16,128]{3,2,1,0:T(8,128)} %off.1) | copy-start | bytes 98308
  1.3 56.8 %copy-start.1 = (f32[2,2,16,128]{3,2,1,0:T(8,128)S(1)}, f32[2,2,16,128]{3,2,1,0:T(8,128)}, u32[]{:S(2)}) copy-start(f32[2,2,16,128]{3,2,1,0:T(8,128)} %vel.1) | copy-start | bytes 98308
  1.3 56.8 %copy-start.2 = (f32[2,16,128]{2,1,0:T(8,128)S(1)}, f32[2,16,128]{2,1,0:T(8,128)}, u32[]{:S(2)}) copy-start(f32[2,16,128]{2,1,0:T(8,128)} %den.1) | copy-start | bytes 49156
  56.2 0.6 %copy-start.5 = (f32[1,128]{1,0:T(1,128)S(1)}, f32[1,128]{1,0:T(1,128)}, u32[]{:S(2)}) copy-start(f32[1,128]{1,0:T(1,128)} %get-tuple-element.31) | copy-start | bytes 1540
  58.1 0.7 %copy-start.4 = (s32[2,16]{1,0:T(2,128)S(1)}, s32[2,16]{1,0:T(2,128)}, u32[]{:S(2)}) copy-start(s32[2,16]{1,0:T(2,128)} %wal.1) | copy-start | bytes 388

commit v3 on v2

--- a/solution.py
+++ b/solution.py
@@ -16,8 +16,14 @@
 BLOCK = 16
 OWN_FIELDS = 5
 CELLS = ROWS * COLS
-PAIRS = CELLS // 2
-RING = 2
+WAYS = 2
+TURNS = CELLS // WAYS
+INNER = COLS - 2
+INNER_TURNS = ROWS * INNER // WAYS
+TILES = 2
+LISTED = ((0, -1), (0, 1), (1, -1), (1, 0), (1, 1), (-1, -1), (-1, 0), (-1, 1))
+NEAR = 5
+PAST = tuple((k, 0 if LISTED[k][1] < 0 else COLS - 1) for k in range(NEAR) if LISTED[k][1] != 0)
 MESH = pl.DeviceIdType.MESH
 
 courant = 0.2
@@ -59,6 +65,22 @@
     )
 
 
+def lane_gather(x, index):
+    return lax.gather(
+        x,
+        index[..., None],
+        lax.GatherDimensionNumbers(
+            offset_dims=(),
+            collapsed_slice_dims=(1,),
+            start_index_map=(1,),
+            operand_batching_dims=(0,),
+            start_indices_batching_dims=(0,),
+        ),
+        slice_sizes=(1, 1),
+        mode=lax.GatherScatterMode.PROMISE_IN_BOUNDS,
+    )
+
+
 def pieces(x):
     high = x.astype(jnp.bfloat16).astype(jnp.float32)
     rest = x - high
@@ -68,13 +90,14 @@
 
 def kernel(
     ring, off, den, vel, cnt, wal, o_off, o_den, o_vel, o_flag,
-    field, rate_t, occ_ref, keep_ref, msg_a, msg_b, slot_a, slot_b,
+    field0, field1, field2, rate_t, occ_ref, keep_ref, msg_a, msg_b, slot_a, slot_b,
     halo_send, halo_recv, a_send, a_recv, b_send, b_recv, *extra,
 ):
     f32 = jnp.float32
+    field = (field0, field1, field2)
     if ring:
-        own_p, pick, bc0, bc1, acc0, acc1, ring0, ring1, code, natural, ranks, box_lo, box_hi, bad = extra
-        bcs, accs, rings = (bc0, bc1), (acc0, acc1), (ring0, ring1)
+        own_p, pick, code, natural, ranks, start, box_lo, box_hi, bad, *ways = extra
+        bcs, accs, lates = [ways[WAYS * n : WAYS * (n + 1)] for n in range(3)]
     else:
         (own_t,) = extra
     gx = lax.axis_index("gx")
@@ -114,11 +137,14 @@
             o_vel[c, a] = vel[c, a] * keep
         o_den[a] = den[a]
     rate_t[...] = jnp.zeros_like(rate_t)
+    for later in field[1:]:
+        later[1 : ROWS + 1, 1 : COLS + 1] = jnp.zeros((ROWS, COLS, FIELDS, SLOTS), f32)
     if ring:
         bad[...] = jnp.zeros_like(bad)
+        natural[...] = jnp.zeros_like(natural)
         r = lax.broadcasted_iota(jnp.int32, pick.shape, 0)
         c = lax.broadcasted_iota(jnp.int32, pick.shape, 1)
-        group = r // COLS
+        group = r // 8
         hit = (group % OWN_FIELDS == c // SLOTS) & (group < 3 * OWN_FIELDS)
         pick[...] = jnp.where(hit, 1.0, 0.0).astype(jnp.bfloat16)
 
@@ -148,22 +174,20 @@
                 occ,
                 jnp.zeros_like(occ),
             ]
-            for f in range(FIELDS):
+            for f in range(FIELDS if s == 0 else 6):
                 for b in range(COLS):
-                    field[s, a + 1, b + 1, f : f + 1, :] = rows[f][b : b + 1]
+                    field[s][a + 1, b + 1, f : f + 1, :] = rows[f][b : b + 1]
             if not ring:
                 own_t[a] = jnp.concatenate(rows, 0).T
 
     def turn():
         for a in range(ROWS):
-            rows = [
-                o_off[0, a] * unit, o_off[1, a] * unit, o_vel[0, a], o_vel[1, a], 10.0 * (o_den[a] - 1.0),
-            ]
+            rows = [o_off[0, a] * unit, o_off[1, a] * unit, o_vel[0, a], o_vel[1, a], 10.0 * (o_den[a] - 1.0)]
             parts = [pieces(x) for x in rows]
-            flat = [p[n] for n in range(3) for p in parts] + [jnp.zeros((COLS, SLOTS), f32)]
-            for n in range(2):
-                half = jnp.concatenate(flat[8 * n : 8 * n + 8], 0)
-                own_p[a, :, n * SLOTS : (n + 1) * SLOTS] = half.T.astype(jnp.bfloat16)
+            for h in range(2):
+                flat = [p[n][8 * h : 8 * h + 8] for n in range(3) for p in parts]
+                flat.append(jnp.zeros((8, SLOTS), f32))
+                own_p[2 * a + h] = jnp.concatenate(flat, 0).T.astype(jnp.bfloat16)
 
     def halo(s):
         copies = []
@@ -172,10 +196,11 @@
             dst_r = pl.ds(1, 2) if a == 0 else (3 if a < 0 else 0)
             src_c = pl.ds(1, COLS) if b == 0 else (1 if b < 0 else COLS)
             dst_c = pl.ds(1, COLS) if b == 0 else (COLS + 1 if b < 0 else 0)
+            sent = slice(0, FIELDS if s == 0 else 6)
             copies.append(
                 pltpu.make_async_remote_copy(
-                    src_ref=field.at[s, src_r, src_c],
-                    dst_ref=field.at[s, dst_r, dst_c],
+                    src_ref=field[s].at[src_r, src_c, sent],
+                    dst_ref=field[s].at[dst_r, dst_c, sent],
                     send_sem=halo_send.at[s, k],
                     recv_sem=halo_recv.at[s, k],
                     device_id=sides[k],
@@ -200,25 +225,32 @@
             device_id=peers[0], device_id_type=MESH,
         )
 
-    def clear_outside(s):
-        zeros_row = jnp.zeros((COLS + 2, FIELDS, SLOTS), f32)
-        zeros_col = jnp.zeros((ROWS + 2, 1, FIELDS, SLOTS), f32)
+    def clear_rows(s):
+        empty = jnp.zeros((COLS, FIELDS, SLOTS), f32)
 
         @pl.when(gx == 0)
         def _():
-            field[s, 0] = zeros_row
+            field[s][0, 1 : COLS + 1] = empty
 
         @pl.when(gx == n_gx - 1)
         def _():
-            field[s, ROWS + 1] = zeros_row
-
-        @pl.when(gy == 0)
-        def _():
-            field[s, :, 0:1] = zeros_col
-
-        @pl.when(gy == n_gy - 1)
-        def _():
-            field[s, :, COLS + 1 : COLS + 2] = zeros_col
+            field[s][ROWS + 1, 1 : COLS + 1] = empty
+
+    def clear_columns(s):
+        empty = jnp.zeros((FIELDS, SLOTS), f32)
+        for at, end in ((0, 0), (ROWS + 1, n_gx - 1)):
+
+            @pl.when(gx == end)
+            def _():
+                field[s][at, 0] = empty
+                field[s][at, COLS + 1] = empty
+
+        for at, end in ((0, 0), (COLS + 1, n_gy - 1)):
+
+            @pl.when(gy == end)
+            def _():
+                for r in range(ROWS + 2):
+                    field[s][r, at] = empty
 
     lanes = lax.broadcasted_iota(jnp.int32, (BLOCK, SLOTS), 1)
     zeros = jnp.zeros((BLOCK, SLOTS), f32)
@@ -235,7 +267,7 @@
                 totals = (zeros, zeros, zeros)
                 for da in range(3):
                     for db in range(3):
-                        rows = [field[s, a + da, b + db, f : f + 1, :] for f in range(6)]
+                        rows = [field[s][a + da, b + db, f : f + 1, :] for f in range(6)]
                         rows[0] = rows[0] + (da - 1) * unit
                         rows[1] = rows[1] + (db - 1) * unit
                         totals = pair_terms(own, rows, totals)
@@ -266,106 +298,203 @@
                 both = within if both is None else both & within
             bad[...] = jnp.maximum(bad[...], jnp.where(inside | both, 0.0, 1.0))
 
-    def lists():
-        def copy_row(t, carry):
-            r = lax.div(t, COLS + 2)
-            c = lax.rem(t, COLS + 2)
-            for n, f in enumerate((0, 1, 2, 3, 6)):
-                natural[n, r, pl.ds(c, 1), :] = field[0, r, c, f : f + 1, :]
-            return carry
-
-        lax.fori_loop(0, (ROWS + 2) * (COLS + 2), copy_row, 0)
+    def near(there, low, high):
+        hit = there[4] > 0.5
+        for d in range(2):
+            way = there[2 + d] * (longest * unit)
+            hit = hit & (there[d] + jnp.maximum(way, 0.0) + margin * unit > low[d])
+            hit = hit & (there[d] + jnp.minimum(way, 0.0) - margin * unit < high[d])
+        return jnp.where(hit, 1.0, 0.0)
+
+    def extents(a):
+        occ = occ_ref[a] > 0.5
         reach = 1.0001
-        masks = []
-        for k, (da, db) in enumerate(SIDES):
-            for a in range(ROWS):
-                there = [natural[n, a + 1 + da, 1 + db : 1 + db + COLS, :] for n in range(5)]
-                near = there[4] > 0.5
-                for d, shift in ((0, da), (1, db)):
-                    occ = occ_ref[a] > 0.5
-                    low = jnp.min(jnp.where(occ, box_lo[d, a], 1e30), axis=1, keepdims=True) - reach
-                    high = jnp.max(jnp.where(occ, box_hi[d, a], -1e30), axis=1, keepdims=True) + reach
-                    x = there[d] + shift * unit
-                    way = there[2 + d] * (longest * unit)
-                    near = near & (x + jnp.maximum(way, 0.0) + margin * unit > low)
-                    near = near & (x + jnp.minimum(way, 0.0) - margin * unit < high)
-                masks.append(jnp.where(near, 1.0, 0.0))
+        low = [jnp.min(jnp.where(occ, box_lo[d, a], 1e30), axis=1, keepdims=True) - reach for d in range(2)]
+        high = [jnp.max(jnp.where(occ, box_hi[d, a], -1e30), axis=1, keepdims=True) + reach for d in range(2)]
+        return low, high
+
+    def beside(a, k, rows):
+        da = LISTED[k][0] * (1 - 2 * a)
+        db = LISTED[k][1]
+        there = [natural[n, a + 1 + da, 1 + db + rows.start : 1 + db + rows.stop, :] for n in range(5)]
+        there[0] = there[0] + da * unit
+        there[1] = there[1] + db * unit
+        return there
+
+    def count_up(masks, at):
         r = lax.broadcasted_iota(jnp.int32, (SLOTS, SLOTS), 0)
         c = lax.broadcasted_iota(jnp.int32, (SLOTS, SLOTS), 1)
         upper = jnp.where(r <= c, 1.0, 0.0).astype(jnp.bfloat16)
         stacked = jnp.concatenate(masks, 0).astype(jnp.bfloat16)
-        ranks[...] = jnp.dot(stacked, upper, preferred_element_type=f32).astype(jnp.int32)
-        where_to = lax.broadcasted_iota(jnp.int32, (8, SLOTS), 1)
-        for g in range(CELLS // 8):
-            base = jnp.zeros((8, 1), jnp.int32)
-            for k in range(8):
-                table = ranks[(k * CELLS + 8 * g) : (k * CELLS + 8 * g + 8), :]
-                count = table[:, SLOTS - 1 : SLOTS]
-                for t in range(RING):
-                    rank = where_to + (SLOTS * t + 1) - base
-                    spot = jnp.zeros((8, SLOTS), jnp.int32)
-                    for bit in (64, 32, 16, 8, 4, 2, 1):
-                        probe = jnp.take_along_axis(table, spot + (bit - 1), axis=1)
-                        spot = jnp.where(probe < rank, spot + bit, spot)
-                    code[t, k, 8 * g : 8 * g + 8, :] = jnp.where((rank >= 1) & (rank <= count), spot, -1)
-                base = base + count
-            over = jnp.where(base > RING * SLOTS, 1.0, 0.0)
-            bad[0:8, :] = jnp.maximum(bad[0:8, :], jnp.broadcast_to(over, (8, SLOTS)))
+        ranks[at : at + stacked.shape[0], :] = jnp.dot(stacked, upper, preferred_element_type=f32).astype(jnp.int32)
+
+    spread_lane = lax.broadcasted_iota(jnp.int32, (8, SLOTS), 1)
+
+    def find(table, base, t):
+        rank = spread_lane + (SLOTS * t + 1) - base
+        spot = jnp.zeros((8, SLOTS), jnp.int32)
+        for bit in (64, 32, 16, 8, 4, 2, 1):
+            probe = lane_gather(table, spot + (bit - 1))
+            spot = jnp.where(probe < rank, spot + bit, spot)
+        return jnp.where((rank >= 1) & (rank <= table[:, SLOTS - 1 : SLOTS]), spot, -1)
+
+    every = slice(0, COLS)
+
+    def lists_near():
+        for a in range(ROWS):
+            whole = [o_off[0, a] * unit, o_off[1, a] * unit, o_vel[0, a], o_vel[1, a], occ_ref[a]]
+            for n in range(5):
+                natural[n, a + 1, 1 : COLS + 1, :] = whole[n]
+        masks = []
+        for a in range(ROWS):
+            low, high = extents(a)
+            masks += [near(beside(a, k, every), low, high) for k in range(NEAR)]
+        count_up(masks, 0)
+        for a in range(ROWS):
+            for g in range(COLS // 8):
+                rows = slice(a * COLS + 8 * g, a * COLS + 8 * g + 8)
+                base = jnp.zeros((8, 1), jnp.int32)
+                for k in range(NEAR):
+                    at = (a * NEAR + k) * COLS + 8 * g
+                    table = ranks[at : at + 8, :]
+                    for t in range(TILES):
+                        code[t, k, rows, :] = find(table, base, t)
+                    base = base + table[:, SLOTS - 1 : SLOTS]
+                start[rows, :] = jnp.broadcast_to(base, (8, SLOTS))
+
+    def flag(over):
+        bad[0:8, :] = jnp.maximum(bad[0:8, :], jnp.broadcast_to(jnp.where(over, 1.0, 0.0), (8, SLOTS)))
+
+    def lists_far():
+        def copy_row(r, c):
+            for n, f in enumerate((0, 1, 2, 3, 6)):
+                natural[n, r, pl.ds(c, 1), :] = field[0][r, c, f : f + 1, :]
+
+        def step(c, carry):
+            copy_row(0, c)
+            copy_row(ROWS + 1, c)
+            return carry
+
+        lax.fori_loop(0, COLS + 2, step, 0)
+        for r in range(1, ROWS + 1):
+            copy_row(r, 0)
+            copy_row(r, COLS + 1)
+        first = ROWS * NEAR * COLS
+        row = lax.broadcasted_iota(jnp.int32, (COLS, 1), 0)
+        masks = []
+        for a in range(ROWS):
+            low, high = extents(a)
+            masks += [near(beside(a, k, every), low, high) for k in range(NEAR, 8)]
+            masks += [jnp.where(row == b, near(beside(a, k, every), low, high), 0.0) for k, b in PAST]
+        count_up(masks, first)
+        width = 8 - NEAR + len(PAST)
+        for a in range(ROWS):
+            for g in range(COLS // 8):
+                rows = slice(a * COLS + 8 * g, a * COLS + 8 * g + 8)
+                base = start[rows, 0:1]
+                for n in range(width):
+                    past = n >= 8 - NEAR
+                    k, b = PAST[n - 8 + NEAR] if past else (NEAR + n, None)
+                    if past and b // 8 != g:
+                        continue
+                    at = first + (a * width + n) * COLS + 8 * g
+                    table = ranks[at : at + 8, :]
+                    for t in range(TILES):
+                        found = find(table, base, t)
+                        if past:
+                            found = jnp.where(found >= 0, found, code[t, k, rows, :])
+                        code[t, k, rows, :] = found
+                    base = base + table[:, SLOTS - 1 : SLOTS]
+                flag(base > TILES * SLOTS)
 
     field_row = lax.broadcasted_iota(jnp.int32, (FIELDS, SLOTS), 0)
 
-    def broadcast_own(c, dst):
-        a = lax.div(c, COLS)
-        b = lax.rem(c, COLS)
-        mine = own_p[a]
-        at = lax.broadcasted_iota(jnp.int32, mine.shape, 1) % COLS
-        mine = jnp.where(at == b, mine.astype(f32), 0.0).astype(jnp.bfloat16)
+    def place(v):
+        if isinstance(v, int):
+            if v < ROWS * INNER:
+                return v // INNER, v % INNER + 1
+            return (v - ROWS * INNER) // 2, (v - ROWS * INNER) % 2 * (COLS - 1)
+        a = jnp.where(v >= INNER, 1, 0)
+        e = v - ROWS * INNER
+        last = e >= 0
+        a = jnp.where(last, lax.shift_right_logical(jnp.maximum(e, 0), 1), a)
+        return a, jnp.where(last, lax.bitwise_and(e, 1) * (COLS - 1), v - INNER * a + 1)
+
+    def broadcast_own(s, c, dst):
+        a, b = place(c)
+        mine = own_p[2 * a + (b // 8 if isinstance(b, int) else lax.shift_right_logical(b, 3))]
+        at = lax.broadcasted_iota(jnp.int32, mine.shape, 1) & 7
+        mine = jnp.where(at == (b & 7), mine.astype(f32), 0.0).astype(jnp.bfloat16)
         wide = jnp.dot(mine, pick[...], preferred_element_type=f32)
         for f in range(OWN_FIELDS):
             dst[f] = wide[:, f * SLOTS : (f + 1) * SLOTS]
 
-    def sweep(bc, acc, tiles, first):
+    def sweep(own_at, start_at, tiles, finish):
         for i0 in range(0, SLOTS, BLOCK):
             here = pl.ds(i0, BLOCK)
-            own = [bc[f, here, :] for f in range(OWN_FIELDS)]
-            totals = (zeros, zeros, zeros) if first else tuple(acc[f, here, :] for f in range(3))
+            own = own_at(here)
+            totals = start_at(here)
             for rows in tiles:
                 totals = pair_terms(own, rows, totals)
+            finish(here, totals)
+
+    def rows_of(tile):
+        return [tile[f : f + 1, :] for f in range(6)]
+
+    def from_zero(here):
+        return zeros, zeros, zeros
+
+    def own_of(bc):
+        return lambda here: [bc[f, here, :] for f in range(OWN_FIELDS)]
+
+    def to_acc(acc):
+        def finish(here, totals):
             for f in range(3):
                 acc[f, here, :] = totals[f]
 
-    def own_pass(s):
-        broadcast_own(0, bc0.at[0])
-
-        def two(u, carry):
-            for n in range(2):
-                c = 2 * u + n
-                a = lax.div(c, COLS)
-                b = lax.rem(c, COLS)
-                later = jnp.minimum(c + 1, CELLS - 1)
-                broadcast_own(later, bcs[1 - n].at[u + n])
-                rows = [field[s, a + 1, b + 1, f : f + 1, :] for f in range(6)]
-                sweep(bcs[n].at[u], accs[n].at[u], [rows], True)
+        return finish
+
+    along_y = [jnp.where(field_row == 1, db * unit, 0.0) for _, db in LISTED]
+
+    def pack(s, c, t, sides_of, packed, inside):
+        a, b = place(c)
+        inward = 1 - 2 * a
+        x_shift = jnp.where(field_row == 0, unit * (inward * 1.0), 0.0)
+        for k in sides_of:
+            way, db = LISTED[k]
+            at_b = b + 1 + db
+            if inside:
+                at_b = jnp.clip(at_b, 1, COLS)
+            take = jnp.broadcast_to(code[t, k, pl.ds(a * COLS + b, 1), :], (FIELDS, SLOTS))
+            moved = lane_gather(field[s][a + 1 + way * inward, at_b], take & (SLOTS - 1))
+            if way > 0:
+                moved = moved + x_shift
+            elif way < 0:
+                moved = moved - x_shift
+            if db:
+                moved = moved + along_y[k]
+            packed = jnp.where(take >= 0, moved, packed)
+        return packed
+
+    nothing = jnp.zeros((FIELDS, SLOTS), f32)
+
+    def early(s):
+        broadcast_own(s, 0, bcs[0].at[0])
+
+        def some(u, carry):
+            for n in range(WAYS):
+                c = WAYS * u + n
+                a, b = place(c)
+                broadcast_own(s, jnp.minimum(c + 1, CELLS - 1), bcs[(n + 1) % WAYS].at[u + (n + 1) // WAYS])
+                rows = [field[s][a + 1, b + 1, f : f + 1, :] for f in range(6)]
+                sweep(own_of(bcs[n].at[u]), from_zero, [rows], to_acc(accs[n].at[u]))
             return carry
 
-        lax.fori_loop(0, PAIRS, two, 0)
-
-    def pack(s, c, dst):
-        a = lax.div(c, COLS)
-        b = lax.rem(c, COLS)
-        for t in range(RING):
-            packed = jnp.zeros((FIELDS, SLOTS), f32)
-            for k, (da, db) in enumerate(SIDES):
-                take = jnp.broadcast_to(code[t, k, pl.ds(c, 1), :], (FIELDS, SLOTS))
-                moved = jnp.take_along_axis(field[s, a + 1 + da, b + 1 + db], take & (SLOTS - 1), axis=1)
-                shift = jnp.where(field_row == 0, da * unit, jnp.where(field_row == 1, db * unit, 0.0))
-                packed = jnp.where(take >= 0, moved + shift, packed)
-            dst[t] = packed
+        lax.fori_loop(0, TURNS, some, 0)
 
     def collect(c, acc, valid):
-        a = lax.div(c, COLS)
-        b = lax.rem(c, COLS)
-        if valid is not None:
+        a, b = place(c)
+        if valid is not True:
             b = jnp.where(valid, b, -4 * SLOTS)
         for i0 in range(0, SLOTS, BLOCK):
             here = pl.ds(i0, BLOCK)
@@ -374,24 +503,41 @@
                 rates = jnp.where(lanes == f * COLS + b, jnp.sum(acc[f, here, :], 1, keepdims=True), rates)
             rate_t[a, here, :] = rates
 
-    def ring_pass(s):
-        for n in range(2):
-            pack(s, n, rings[n].at[0])
-
-        def two(u, carry):
-            for n in range(2):
-                c = 2 * u + n
+    def late(s, relay, rest_of_halo):
+        def pack_all(c, dst):
+            for t in range(TILES):
+                dst[t] = pack(s, c, t, range(8), nothing, False)
+
+        def begin(u):
+            for n in range(WAYS):
+                pack_all(WAYS * u + n, lates[n].at[u])
+
+        def some(last, u, carry):
+            for n in range(WAYS):
+                c = WAYS * u + n
                 if n == 0:
-                    collect(jnp.maximum(c - 1, 0), acc1.at[jnp.maximum(u - 1, 0)], c > 0)
+                    w = jnp.maximum(u - 1, 0)
+                    collect(jnp.maximum(c - 1, 0), accs[WAYS - 1].at[w], u > 0)
                 else:
-                    collect(c - 1, acc0.at[u], None)
-                tiles = [[rings[n][u, t, f : f + 1, :] for f in range(6)] for t in range(RING)]
-                sweep(bcs[n].at[u], accs[n].at[u], tiles, False)
-                pack(s, jnp.minimum(c + 2, CELLS - 1), rings[n].at[u + 1])
+                    collect(c - 1, accs[n - 1].at[u], True)
+                tiles = [rows_of(lates[n].at[u, t]) for t in range(TILES)]
+                acc = accs[n].at[u]
+
+                def start_at(here):
+                    return tuple(acc[f, here, :] for f in range(3))
+
+                sweep(own_of(bcs[n].at[u]), start_at, tiles, to_acc(acc))
+                pack_all(jnp.minimum(c + WAYS, last - WAYS + n), lates[n].at[u + 1])
             return carry
 
-        lax.fori_loop(0, PAIRS, two, 0)
-        collect(CELLS - 1, acc1.at[PAIRS - 1], None)
+        begin(0)
+        lax.fori_loop(0, 2, functools.partial(some, ROWS * INNER), 0)
+        relay()
+        lax.fori_loop(2, INNER_TURNS, functools.partial(some, ROWS * INNER), 0)
+        rest_of_halo()
+        begin(INNER_TURNS)
+        lax.fori_loop(INNER_TURNS, TURNS, functools.partial(some, CELLS), 0)
+        collect(CELLS - 1, accs[WAYS - 1].at[TURNS - 1], True)
 
     def update(s, step):
         for a in range(ROWS):
@@ -413,30 +559,52 @@
     me_b = plane
     for s in range(ITERS):
         fastest(s)
+        copies = halo(s)
         if s == 0:
+            publish(s)
+            if ring:
+                boxes()
+                lists_near()
+                turn()
             pl.semaphore_wait(barrier, len(peers_a) + len(peers_b) + len(sides))
-        spread(s, peers_a, msg_a, slot_a, me_a, a_send, a_recv)
-        publish(s)
-        copies = halo(s)
+            spread(s, peers_a, msg_a, slot_a, me_a, a_send, a_recv)
+        else:
+            spread(s, peers_a, msg_a, slot_a, me_a, a_send, a_recv)
+            publish(s)
         for copy in copies:
             copy.start()
         if ring:
-            if s == 0:
-                boxes()
-            turn()
-            own_pass(s)
-        gathered(s, peers_a, slot_a, a_send, a_recv).wait_recv()
-        msg_b[s] = jnp.max(slot_a[s], axis=0)
-        spread(s, peers_b, msg_b, slot_b, me_b, b_send, b_recv)
-        for copy in copies:
-            copy.wait_recv()
-        clear_outside(s)
-        if ring:
-            if s == 0:
-                lists()
-            ring_pass(s)
+            if s > 0:
+                turn()
+            early(s)
+
+        def relay():
+            gathered(s, peers_a, slot_a, a_send, a_recv).wait_recv()
+            msg_b[s] = jnp.max(slot_a[s], axis=0)
+            spread(s, peers_b, msg_b, slot_b, me_b, b_send, b_recv)
+
+        if s == 0 or not ring:
+            relay()
+        for copy, (a, b) in zip(copies, SIDES):
+            if b == 0:
+                copy.wait_recv()
+        clear_rows(s)
+
+        def rest_of_halo():
+            for copy, (a, b) in zip(copies, SIDES):
+                if b != 0:
+                    copy.wait_recv()
+            clear_columns(s)
+
+        if not ring:
+            rest_of_halo()
+            dense(s)
+        elif s == 0:
+            rest_of_halo()
+            lists_far()
+            late(s, lambda: None, lambda: None)
         else:
-            dense(s)
+            late(s, relay, rest_of_halo)
         gathered(s, peers_b, slot_b, b_send, b_recv).wait_recv()
         result = jnp.max(slot_b[s], axis=0)
         top = 10.0 + jnp.sqrt(result[:, 0:1])
@@ -457,21 +625,18 @@
     n_a, n_b = 2 * n_gx, n_gy // 2
     if ring:
         extra = [
-            pltpu.VMEM((ROWS, SLOTS, 2 * SLOTS), jnp.bfloat16),
-            pltpu.VMEM((2 * SLOTS, OWN_FIELDS * SLOTS), jnp.bfloat16),
-            pltpu.VMEM((PAIRS + 1, OWN_FIELDS, SLOTS, SLOTS), f32),
-            pltpu.VMEM((PAIRS + 1, OWN_FIELDS, SLOTS, SLOTS), f32),
-            pltpu.VMEM((PAIRS, 3, SLOTS, SLOTS), f32),
-            pltpu.VMEM((PAIRS, 3, SLOTS, SLOTS), f32),
-            pltpu.VMEM((PAIRS + 1, RING, FIELDS, SLOTS), f32),
-            pltpu.VMEM((PAIRS + 1, RING, FIELDS, SLOTS), f32),
-            pltpu.VMEM((RING, 8, CELLS, SLOTS), jnp.int32),
+            pltpu.VMEM((2 * ROWS, SLOTS, SLOTS), jnp.bfloat16),
+            pltpu.VMEM((SLOTS, OWN_FIELDS * SLOTS), jnp.bfloat16),
+            pltpu.VMEM((TILES, 8, CELLS, SLOTS), jnp.int32),
             pltpu.VMEM((5, ROWS + 2, 24, SLOTS), f32),
-            pltpu.VMEM((8 * CELLS, SLOTS), jnp.int32),
+            pltpu.VMEM((ROWS * (8 + len(PAST)) * COLS, SLOTS), jnp.int32),
+            pltpu.VMEM((CELLS, SLOTS), jnp.int32),
             pltpu.VMEM((2, ROWS, COLS, SLOTS), f32),
             pltpu.VMEM((2, ROWS, COLS, SLOTS), f32),
             pltpu.VMEM((COLS, SLOTS), f32),
         ]
+        for per_cell in ((OWN_FIELDS, SLOTS, SLOTS), (3, SLOTS, SLOTS), (TILES, FIELDS, SLOTS)):
+            extra += [pltpu.VMEM((TURNS + 1,) + per_cell, f32)] * WAYS
     else:
         extra = [pltpu.VMEM((ROWS, SLOTS, SLOTS), f32)]
     return pl.pallas_call(
@@ -485,7 +650,9 @@
         in_specs=[pl.BlockSpec(memory_space=pltpu.VMEM)] * 5,
         out_specs=tuple(pl.BlockSpec(memory_space=pltpu.VMEM) for _ in range(4)),
         scratch_shapes=[
-            pltpu.VMEM((ITERS, ROWS + 2, COLS + 2, FIELDS, SLOTS), f32),
+            pltpu.VMEM((ROWS + 2, COLS + 2, FIELDS, SLOTS), f32),
+            pltpu.VMEM((ROWS + 2, COLS + 2, FIELDS, SLOTS), f32),
+            pltpu.VMEM((ROWS + 2, COLS + 2, FIELDS, SLOTS), f32),
             pltpu.VMEM((ROWS, SLOTS, SLOTS), f32),
             pltpu.VMEM((ROWS, COLS, SLOTS), f32),
             pltpu.VMEM((ROWS, COLS, SLOTS), f32),

time: 60.8 us -> 57.8 us (0.951)
  Pallas kernels: 54.9 us -> 51.9 us
    pallas_call x1, Pallas kernels: 54.9 us -> 51.9 us  [substeps(): pl.pallas_call(functools.partial(kernel, ring), out_shape=(shape(offsets....]
where the time goes in v3:
time: 57.8 us; the launch traced here: 57.6 us
  Pallas kernels  51.9 us (90%)
  local copies, waits for them, and re-layouts  4.36 us (8%)
  between operations  1.34 us (2%)
    pallas_call x1, Pallas kernels, substeps(): pl.pallas_call(functools.partial(kernel, ring), out_shape=(shape(offsets....  51.9 us
    unnamed x15, local copies, waits for them, and re-layouts  3.78 us

profile of v3, /device:TPU:1, one launch (start us, length us, event | category | flops | bytes accessed | tf_op | source)
XLA Modules:
  0.0 57.6 jit_solution(6529505448304986022)
XLA Ops:
  0.6 0.0 copy-start.3
  0.6 0.7 %copy-done.3 = s32[2,16]{1,0:T(2,128)S(1)} copy-done((s32[2,16]{1,0:T(2,128)S(1)}, s32[2,16]{1,0:T(2,128)}, u32[]{:S(2)}) %copy-start.3) | copy-done | bytes 152
  1.3 0.0 copy-start
  1.3 0.0 copy-start.1
  1.3 0.0 copy-start.2
  1.3 51.9 %shard_map.82 = (f32[2,2,16,128]{3,2,1,0:T(8,128)S(1)}, f32[2,16,128]{2,1,0:T(8,128)S(1)}, f32[2,2,16,128]{3,2,1,0:T(8,128)S(1)}, f32[1,128]{1,0:T(1,128)}) custom-call(f32[2,2,16,128]{3,2,1,0:T(8,128)} %off.1, f32[2,16,128]{2,1,0:T(8,128)} %den.1, f32[2,2,16,128]{3,2,1,0:T(8,128)} %vel.1, s32[2,16]{1,0:T(2,128)S(1)} %copy-done.3, s32[2,16]{1,0:T(2,128)} %wal.1), custom_call_target="tpu_custom_call" | custom-call | tf_op jit(solution)/shard_map/pallas_call | solution.py:642
  53.2 0.0 copy-start.5
  53.2 0.6 %copy-done.5 = f32[1,128]{1,0:T(1,128)S(1)} copy-done((f32[1,128]{1,0:T(1,128)S(1)}, f32[1,128]{1,0:T(1,128)}, u32[]{:S(2)}) %copy-start.5) | copy-done | bytes 536
  53.8 0.6 %slice.3 = f32[1,1]{1,0:T(1,128)} slice(f32[1,128]{1,0:T(1,128)S(1)} %copy-done.5), slice={[0:1], [127:128]} | slice | bytes 8 | tf_op jit(solution)/shard_map/slice | solution.py:678
  55.1 0.0 copy-start.4
  55.1 0.0 copy-done
  55.1 0.0 copy-done.1
  55.1 0.0 copy-done.2
  55.1 0.6 %copy-done.4 = s32[2,16]{1,0:T(2,128)S(1)} copy-done((s32[2,16]{1,0:T(2,128)S(1)}, s32[2,16]{1,0:T(2,128)}, u32[]{:S(2)}) %copy-start.4) | copy-done | bytes 152
  55.7 0.6 %copy.23 = f32[2,2,16,128]{3,2,1,0:T(8,128)} copy(f32[2,2,16,128]{3,2,1,0:T(8,128)S(1)} %get-tuple-element.50) | data formatting | bytes 65536
  56.4 0.6 %copy.24 = f32[2,16,128]{2,1,0:T(8,128)} copy(f32[2,16,128]{2,1,0:T(8,128)S(1)} %get-tuple-element.51) | data formatting | bytes 32768
  57.0 0.6 %copy.25 = f32[2,2,16,128]{3,2,1,0:T(8,128)} copy(f32[2,2,16,128]{3,2,1,0:T(8,128)S(1)} %get-tuple-element.52) | data formatting | bytes 65536
  (1 shorter events, 0.0 us)
Async XLA Ops:
  0.6 0.7 %copy-start.3 = (s32[2,16]{1,0:T(2,128)S(1)}, s32[2,16]{1,0:T(2,128)}, u32[]{:S(2)}) copy-start(s32[2,16]{1,0:T(2,128)} %cnt.1) | copy-start | bytes 388
  1.3 53.8 %copy-start = (f32[2,2,16,128]{3,2,1,0:T(8,128)S(1)}, f32[2,2,16,128]{3,2,1,0:T(8,128)}, u32[]{:S(2)}) copy-start(f32[2,2,16,128]{3,2,1,0:T(8,128)} %off.1) | copy-start | bytes 98308
  1.3 53.8 %copy-start.1 = (f32[2,2,16,128]{3,2,1,0:T(8,128)S(1)}, f32[2,2,16,128]{3,2,1,0:T(8,128)}, u32[]{:S(2)}) copy-start(f32[2,2,16,128]{3,2,1,0:T(8,128)} %vel.1) | copy-start | bytes 98308
  1.3 53.8 %copy-start.2 = (f32[2,16,128]{2,1,0:T(8,128)S(1)}, f32[2,16,128]{2,1,0:T(8,128)}, u32[]{:S(2)}) copy-start(f32[2,16,128]{2,1,0:T(8,128)} %den.1) | copy-start | bytes 49156
  53.2 0.6 %copy-start.5 = (f32[1,128]{1,0:T(1,128)S(1)}, f32[1,128]{1,0:T(1,128)}, u32[]{:S(2)}) copy-start(f32[1,128]{1,0:T(1,128)} %get-tuple-element.31) | copy-start | bytes 1540
  55.1 0.7 %copy-start.4 = (s32[2,16]{1,0:T(2,128)S(1)}, s32[2,16]{1,0:T(2,128)}, u32[]{:S(2)}) copy-start(s32[2,16]{1,0:T(2,128)} %wal.1) | copy-start | bytes 388
